TPU v7x, 256 devices: a whole 4x4x8 slice. The times are simulated.
256 devices in a mesh: tm: 32 (over y, x, core), rows: 8 (over z).
Axes of the slice: x: 4, y: 4, z: 8, core: 2. Of those that a mesh axis runs over, the one named last changes fastest.
Arguments:
- frames: bfloat16 [512, 8, 128, 128], P('tm', 'rows'), may hold values from 0.25 to 4
- block_owner: int32 [8, 128, 1], replicated, may hold values from 0 to 31; in each aligned block of 128 rows (0 to 127, 128 to 255, ..., all dimensions but the last counted through in order) at most 12 rows name the same one
- cycle_slot: int32 [8, 128], replicated, may hold values from 0 to 1
- lag_table: int32 [4, 8], replicated, may hold values from 1 to 8
Outputs:
- g2: float32 [8, 32, 128, 128], P('rows', None, 'tm')
- two_time: float32 [512, 64, 512], P('rows', 'tm')
Inputs may be any that keep to these rules, and one draw needn't show every extreme that they name: `block_owner`: in each row group no owner gets more than 12 blocks; some owner gets exactly 12 in some groups.
All inputs are finite; a program needn't handle non-finite values.
Results may differ from a plain program's by a relative error of at most 0.0003.
Values may be sent and summed in bfloat16 or wider, within the bound.
A program may use at most 64 MiB of HBM per device.

v0:
```python
import jax
import jax.numpy as jnp
from jax import lax
from jax.sharding import PartitionSpec as P

CYCLES = 64
LEVELS = 4
LAGMAX = 8


def multitau(series, lag_table):
    results = []
    current = series
    for level in range(LEVELS):
        length = current.shape[0]
        padded = jnp.concatenate(
            [current, jnp.zeros((LAGMAX,) + current.shape[1:], current.dtype)], 0
        )
        positions = jnp.arange(length, dtype=jnp.int32)

        def single_lag(lag, current=current, padded=padded, length=length, positions=positions):
            shifted = lax.dynamic_slice_in_dim(padded, lag, length, 0).astype(jnp.float32)
            base = current.astype(jnp.float32)
            valid = (positions < length - lag)[:, None, None]
            count = (length - lag).astype(jnp.float32)
            first = jnp.sum(jnp.where(valid, base, jnp.float32(0.0)), 0)
            second = jnp.sum(shifted, 0)
            product = jnp.sum(jnp.where(valid, base * shifted, jnp.float32(0.0)), 0)
            denom = first * second
            safe = jnp.where(denom > 0, denom, jnp.float32(1.0))
            return jnp.where(denom > 0, product * count / safe, jnp.float32(0.0))

        results.append(lax.map(single_lag, lag_table[level]))
        if level + 1 < LEVELS:
            base = current.astype(jnp.float32)
            current = (base[0::2] + base[1::2]) * 0.5
    return jnp.concatenate(results, 0)


def shards(frames, block_owner, cycle_slot, lag_table):
    local = frames[:, 0]
    width = local.shape[2]
    nblocks = local.shape[1]
    ntm = lax.axis_size("tm")
    nrows = lax.axis_size("rows")
    me_tm = lax.axis_index("tm")
    me_row = lax.axis_index("rows")
    slot_capacity = 3 * nblocks // ntm
    cycle_dev = CYCLES // ntm
    owners_all = block_owner[:, :, 0]
    owners = lax.dynamic_index_in_dim(owners_all, me_row, 0, False)
    slots = lax.dynamic_index_in_dim(cycle_slot, me_row, 0, False)
    onehot = (owners[:, None] == jnp.arange(ntm, dtype=jnp.int32)[None, :]).astype(jnp.int32)
    rank = jnp.sum((jnp.cumsum(onehot, 0) - onehot) * onehot, 1)
    match = (owners[None, None, :] == jnp.arange(ntm, dtype=jnp.int32)[:, None, None]) & (
        rank[None, None, :] == jnp.arange(slot_capacity, dtype=jnp.int32)[None, :, None]
    )
    source = jnp.sum(jnp.where(match, jnp.arange(nblocks, dtype=jnp.int32)[None, None, :], 0), 2)
    filled = jnp.any(match, 2)
    packed = jnp.take(local, source.reshape(-1), axis=1) * filled.reshape(-1)[None, :, None].astype(
        jnp.bfloat16
    )
    owned_blocks = lax.all_to_all(packed, "tm", split_axis=1, concat_axis=0, tiled=True)
    nframes = owned_blocks.shape[0]
    span = nframes // nrows
    mine_source = lax.dynamic_index_in_dim(source, me_tm, 0, False)
    mine_filled = lax.dynamic_index_in_dim(filled, me_tm, 0, False)
    slot_cycle = jnp.take(slots, mine_source)
    masks = (
        mine_filled[None, :]
        & (slot_cycle[None, :] == jnp.arange(cycle_dev, dtype=jnp.int32)[:, None])
    ).astype(jnp.float32)
    block_totals = jnp.sum(owned_blocks.astype(jnp.float32), 2)
    partial_sums = jnp.dot(masks, block_totals.T, precision=lax.Precision.HIGHEST)
    sums = lax.psum(partial_sums, "rows")
    mask_words = masks.astype(jnp.bfloat16)
    masked_pixels = owned_blocks[:, None] * mask_words[None, :, :, None]
    gram = lax.psum_scatter(
        jnp.einsum(
            "adib,jib->adj", masked_pixels, owned_blocks, preferred_element_type=jnp.float32
        ),
        "rows",
        scatter_dimension=0,
        tiled=True,
    )
    cycles_all = owners_all * cycle_dev + cycle_slot
    mine_cycles = me_tm * cycle_dev + jnp.arange(cycle_dev, dtype=jnp.int32)
    counts = width * jnp.sum(
        (cycles_all[:, :, None] == mine_cycles[None, None, :]).astype(jnp.float32), (0, 1)
    )
    first_sums = lax.dynamic_slice_in_dim(sums, me_row * span, span, 1).T
    denom = jnp.maximum(first_sums[:, :, None] * sums[None, :, :], jnp.float32(1.0))
    two_time = counts[None, :, None] * gram / denom
    owner_corr = multitau(owned_blocks, lag_table)
    own_mask = (owners == me_tm).astype(jnp.float32)
    outgoing = (
        jnp.take(owner_corr, jnp.minimum(rank, slot_capacity - 1), axis=1) * own_mask[None, :, None]
    )
    returned = lax.all_to_all(outgoing, "tm", split_axis=1, concat_axis=0, tiled=True)
    g2 = jnp.sum(returned.reshape(ntm, owner_corr.shape[0], nblocks // ntm, width), 0)
    return (g2[None], two_time)


def solution(mesh):
    in_specs = (P("tm", "rows", None, None), P(), P(), P())
    out_specs = (P("rows", None, "tm", None), P("rows", "tm", None))
    return jax.shard_map(shards, mesh=mesh, in_specs=in_specs, out_specs=out_specs, check_vma=False)
```

profile of v0, /device:TPU:2, one launch (start us, length us, event | category | flops | bytes accessed | tf_op | source)
XLA Modules:
  0.0 394.1 jit_solution(12015605194849971110)
XLA Ops:
  9.5 1.4 copy.152
  10.8 1.9 gather_fusion
  12.8 2.9 multiply_bitcast_fusion.1
  15.7 7.7 %all-to-all-start = ((bf16[16,384,128]{2,0,1:T(8,128)(2,1)}), bf16[16,384,128]{2,0,1:T(8,128)(2,1)S(1)}, u32[]{:S(2)}, u32[]{:S(2)}) async-start(bf16[16,384,128]{2,0,1:T(8,128)(2,1)} %multiply_bitcast_fusion.1), calls=%async_computation | async-start | bytes 3145728 | tf_op jit(solution)/shard_map/all_to_all | solution.py:63
  27.3 18.1 %all-to-all-done = bf16[16,384,128]{2,0,1:T(8,128)(2,1)S(1)} async-done(((bf16[16,384,128]{2,0,1:T(8,128)(2,1)}), bf16[16,384,128]{2,0,1:T(8,128)(2,1)S(1)}, u32[]{:S(2)}, u32[]{:S(2)}) %all-to-all-start) | async-done | bytes 1572896 | tf_op jit(solution)/shard_map/all_to_all | solution.py:63
  47.0 2.1 bitcast_convert_fusion
  49.1 6.0 %slice.33 = f32[256,12,128]{2,0,1:T(8,128)S(1)} slice(f32[512,12,128]{2,0,1:T(8,128)} %bitcast_convert_fusion), slice={[1:512:2], [0:12:1], [0:128:1]} | slice | bytes 3145728 | tf_op jit(solution)/shard_map/slice | solution.py:36
  55.1 7.6 %slice.32 = f32[256,12,128]{2,0,1:T(8,128)} slice(f32[512,12,128]{2,0,1:T(8,128)} %bitcast_convert_fusion), slice={[0:512:2], [0:12:1], [0:128:1]} | slice | bytes 3145728 | tf_op jit(solution)/shard_map/slice | solution.py:36
  62.7 1.7 add_multiply_fusion
  64.6 2.4 slice.35
  69.2 1.4 slice.38
  70.6 1.7 copy.99
  73.7 2.4 copy.95
  77.4 3.2 fusion.23
  81.2 118.2 %while.44 = (s32[]{:T(128)}, f32[8,12,128]{2,0,1:T(8,128)}, s32[8]{0:T(128)}, bf16[512,12,128]{2,1,0:T(8,128)(2,1)}, bf16[520,12,128]{2,0,1:T(8,128)(2,1)}, /*index=5*/s32[]{:T(128)}, s32[]{:T(128)}, s32[]{:T(128)}, s32[]{:T(128)}) while((s32[]{:T(128)}, f32[8,12,128]{2,0,1:T(8,128)}, s32[8]{0:T(128)}, ...), condition=%wide.region_8.9_spmd.clone, body=%wide.region_4.8_spmd.clone.sunk | while | flops 6296583 | bytes 12651731 | solution.py:33
  84.5 2.0 constant_dynamic-slice_fusion.11
  86.6 7.9 %fusion.49 = (f32[12,128]{1,0:T(8,128)S(1)}, f32[12,128]{1,0:T(8,128)S(1)}, f32[12,128]{1,0:T(8,128)S(1)}) fusion(bf16[512,12,128]{2,1,0:T(8,128)(2,1)S(1)} %copy-done, pred[512]{0:T(512)(128)(4,1)S(1)} %iota_compare_fusion.11, bf16[512,12,128]{2,0,1:T(8,128)(2,1)S(1)} %constant_dynamic-slice_fusion.11), kind=kLoop, calls=%fused_computation.10.clone.1 | loop fusion | flops 6286848 | bytes 3164672 | tf_op jit(solution)/shard_map/while/body/eval_jaxpr/reduce_sum | solution.py:26
  94.5 1.4 dynamic_update_slice.21
  99.3 2.0 constant_dynamic-slice_fusion.11
  101.4 7.9 %fusion.49 = (f32[12,128]{1,0:T(8,128)S(1)}, f32[12,128]{1,0:T(8,128)S(1)}, f32[12,128]{1,0:T(8,128)S(1)}) fusion(bf16[512,12,128]{2,1,0:T(8,128)(2,1)S(1)} %copy-done, pred[512]{0:T(512)(128)(4,1)S(1)} %iota_compare_fusion.11, bf16[512,12,128]{2,0,1:T(8,128)(2,1)S(1)} %constant_dynamic-slice_fusion.11), kind=kLoop, calls=%fused_computation.10.clone.1 | loop fusion | flops 6286848 | bytes 3164672 | tf_op jit(solution)/shard_map/while/body/eval_jaxpr/reduce_sum | solution.py:26
  109.3 1.4 dynamic_update_slice.21
  114.1 2.0 constant_dynamic-slice_fusion.11
  116.2 7.9 %fusion.49 = (f32[12,128]{1,0:T(8,128)S(1)}, f32[12,128]{1,0:T(8,128)S(1)}, f32[12,128]{1,0:T(8,128)S(1)}) fusion(bf16[512,12,128]{2,1,0:T(8,128)(2,1)S(1)} %copy-done, pred[512]{0:T(512)(128)(4,1)S(1)} %iota_compare_fusion.11, bf16[512,12,128]{2,0,1:T(8,128)(2,1)S(1)} %constant_dynamic-slice_fusion.11), kind=kLoop, calls=%fused_computation.10.clone.1 | loop fusion | flops 6286848 | bytes 3164672 | tf_op jit(solution)/shard_map/while/body/eval_jaxpr/reduce_sum | solution.py:26
  124.1 1.4 dynamic_update_slice.21
  128.9 2.0 constant_dynamic-slice_fusion.11
  131.0 7.9 %fusion.49 = (f32[12,128]{1,0:T(8,128)S(1)}, f32[12,128]{1,0:T(8,128)S(1)}, f32[12,128]{1,0:T(8,128)S(1)}) fusion(bf16[512,12,128]{2,1,0:T(8,128)(2,1)S(1)} %copy-done, pred[512]{0:T(512)(128)(4,1)S(1)} %iota_compare_fusion.11, bf16[512,12,128]{2,0,1:T(8,128)(2,1)S(1)} %constant_dynamic-slice_fusion.11), kind=kLoop, calls=%fused_computation.10.clone.1 | loop fusion | flops 6286848 | bytes 3164672 | tf_op jit(solution)/shard_map/while/body/eval_jaxpr/reduce_sum | solution.py:26
  138.9 1.4 dynamic_update_slice.21
  143.7 2.0 constant_dynamic-slice_fusion.11
  145.7 7.9 %fusion.49 = (f32[12,128]{1,0:T(8,128)S(1)}, f32[12,128]{1,0:T(8,128)S(1)}, f32[12,128]{1,0:T(8,128)S(1)}) fusion(bf16[512,12,128]{2,1,0:T(8,128)(2,1)S(1)} %copy-done, pred[512]{0:T(512)(128)(4,1)S(1)} %iota_compare_fusion.11, bf16[512,12,128]{2,0,1:T(8,128)(2,1)S(1)} %constant_dynamic-slice_fusion.11), kind=kLoop, calls=%fused_computation.10.clone.1 | loop fusion | flops 6286848 | bytes 3164672 | tf_op jit(solution)/shard_map/while/body/eval_jaxpr/reduce_sum | solution.py:26
  153.7 1.4 dynamic_update_slice.21
  158.5 2.0 constant_dynamic-slice_fusion.11
  160.5 7.9 %fusion.49 = (f32[12,128]{1,0:T(8,128)S(1)}, f32[12,128]{1,0:T(8,128)S(1)}, f32[12,128]{1,0:T(8,128)S(1)}) fusion(bf16[512,12,128]{2,1,0:T(8,128)(2,1)S(1)} %copy-done, pred[512]{0:T(512)(128)(4,1)S(1)} %iota_compare_fusion.11, bf16[512,12,128]{2,0,1:T(8,128)(2,1)S(1)} %constant_dynamic-slice_fusion.11), kind=kLoop, calls=%fused_computation.10.clone.1 | loop fusion | flops 6286848 | bytes 3164672 | tf_op jit(solution)/shard_map/while/body/eval_jaxpr/reduce_sum | solution.py:26
  168.4 1.4 dynamic_update_slice.21
  173.2 2.0 constant_dynamic-slice_fusion.11
  175.3 7.9 %fusion.49 = (f32[12,128]{1,0:T(8,128)S(1)}, f32[12,128]{1,0:T(8,128)S(1)}, f32[12,128]{1,0:T(8,128)S(1)}) fusion(bf16[512,12,128]{2,1,0:T(8,128)(2,1)S(1)} %copy-done, pred[512]{0:T(512)(128)(4,1)S(1)} %iota_compare_fusion.11, bf16[512,12,128]{2,0,1:T(8,128)(2,1)S(1)} %constant_dynamic-slice_fusion.11), kind=kLoop, calls=%fused_computation.10.clone.1 | loop fusion | flops 6286848 | bytes 3164672 | tf_op jit(solution)/shard_map/while/body/eval_jaxpr/reduce_sum | solution.py:26
  183.2 1.4 dynamic_update_slice.21
  188.0 2.0 constant_dynamic-slice_fusion.11
  190.1 7.9 %fusion.49 = (f32[12,128]{1,0:T(8,128)S(1)}, f32[12,128]{1,0:T(8,128)S(1)}, f32[12,128]{1,0:T(8,128)S(1)}) fusion(bf16[512,12,128]{2,1,0:T(8,128)(2,1)S(1)} %copy-done, pred[512]{0:T(512)(128)(4,1)S(1)} %iota_compare_fusion.11, bf16[512,12,128]{2,0,1:T(8,128)(2,1)S(1)} %constant_dynamic-slice_fusion.11), kind=kLoop, calls=%fused_computation.10.clone.1 | loop fusion | flops 6286848 | bytes 3164672 | tf_op jit(solution)/shard_map/while/body/eval_jaxpr/reduce_sum | solution.py:26
  198.0 1.4 dynamic_update_slice.21
  203.4 40.9 %while.46 = (s32[]{:T(128)}, f32[8,12,128]{2,0,1:T(8,128)S(1)}, s32[8]{0:T(128)S(1)}, f32[128,12,128]{2,1,0:T(8,128)S(1)}, f32[136,12,128]{2,0,1:T(8,128)}, /*index=5*/s32[]{:T(128)}, s32[]{:T(128)}, s32[]{:T(128)}, s32[]{:T(128)}) while((s32[]{:T(128)}, f32[8,12,128]{2,0,1:T(8,128)S(1)}, s32[8]{0:T(128)S(1)}, ...), condition=%wide.region_18.19_spmd.clone, body=%wide.region_14.18_spmd.clone.sunk | while | flops 1184391 | bytes 3213751 | solution.py:33
  244.3 2.7 concatenate.16
  247.0 69.4 %while.45 = (s32[]{:T(128)}, f32[8,12,128]{2,0,1:T(8,128)S(1)}, s32[8]{0:T(128)S(1)}, f32[256,12,128]{2,1,0:T(8,128)S(1)}, f32[264,12,128]{2,0,1:T(8,128)}, /*index=5*/s32[]{:T(128)}, s32[]{:T(128)}, s32[]{:T(128)}, s32[]{:T(128)}) while((s32[]{:T(128)}, f32[8,12,128]{2,0,1:T(8,128)S(1)}, s32[8]{0:T(128)S(1)}, ...), condition=%wide.region_13.14_spmd.clone, body=%wide.region_9.13_spmd.clone.sunk | while | flops 2364167 | bytes 6359735 | solution.py:33
  250.4 1.6 fusion.50
  252.1 3.5 select_reduce_fusion.8
  259.1 1.6 fusion.50
  260.8 3.5 select_reduce_fusion.8
  267.8 1.6 fusion.50
  269.4 3.5 select_reduce_fusion.8
  276.5 1.6 fusion.50
  278.1 3.5 select_reduce_fusion.8
  285.2 1.6 fusion.50
  286.8 3.5 select_reduce_fusion.8
  293.8 1.6 fusion.50
  295.5 3.5 select_reduce_fusion.8
  302.5 1.6 fusion.50
  304.2 3.5 select_reduce_fusion.8
  311.2 1.6 fusion.50
  312.9 3.5 select_reduce_fusion.8
  316.5 29.1 %while.47 = (s32[]{:T(128)}, f32[8,12,128]{2,0,1:T(8,128)S(1)}, s32[8]{0:T(128)S(1)}, f32[64,12,128]{2,1,0:T(8,128)S(1)}, f32[72,12,128]{2,0,1:T(8,128)S(1)}, /*index=5*/s32[]{:T(128)}, s32[]{:T(128)}, s32[]{:T(128)}, s32[]{:T(128)}) while((s32[]{:T(128)}, f32[8,12,128]{2,0,1:T(8,128)S(1)}, s32[8]{0:T(128)S(1)}, ...), condition=%wide.region_23.24_spmd.clone, body=%wide.region_19.23_spmd.clone.sunk | while | flops 594503 | bytes 1640759 | solution.py:33
  346.5 1.7 multiply_bitcast_fusion
  348.2 6.6 %all-to-all-start.1 = ((f32[32,128,128]{2,0,1:T(8,128)}), f32[32,128,128]{2,0,1:T(8,128)}, u32[]{:S(2)}, u32[]{:S(2)}) async-start(f32[32,128,128]{2,0,1:T(8,128)} %multiply_bitcast_fusion), calls=%async_computation.1 | async-start | bytes 4194304 | tf_op jit(solution)/shard_map/all_to_all | solution.py:99
  356.3 20.0 %psum.7 = f32[2,512]{1,0:T(2,128)S(1)} all-reduce(f32[2,512]{1,0:T(2,128)S(1)} %fusion.32), channel_id=1, replica_groups=mesh['tm'=32,'rows'=8] {'rows'}, use_global_device_ids=true, to_apply=%region_28.29 | all-reduce | flops 1024 | bytes 8192 | tf_op jit(solution)/shard_map/psum | solution.py:75
  376.4 6.5 %all-to-all-done.1 = f32[32,128,128]{2,0,1:T(8,128)} async-done(((f32[32,128,128]{2,0,1:T(8,128)}), f32[32,128,128]{2,0,1:T(8,128)}, u32[]{:S(2)}, u32[]{:S(2)}) %all-to-all-start.1) | async-done | bytes 2097184 | tf_op jit(solution)/shard_map/all_to_all | solution.py:99
  382.9 1.7 reduce_sum.157
  (308 shorter events, 66.8 us)
Async XLA Ops:
  15.7 9.7 %copy-start.12 = (s32[8,128,1]{1,2,0:T(1,128)S(1)}, s32[8,128,1]{1,2,0:T(1,128)}, u32[]{:S(2)}) copy-start(s32[8,128,1]{1,2,0:T(1,128)} %param.13) | copy-start | bytes 12292
  15.7 11.0 %copy-start.19 = (s32[4,8]{1,0:T(4,128)S(1)}, s32[4,8]{1,0:T(4,128)}, u32[]{:S(2)}) copy-start(s32[4,8]{1,0:T(4,128)} %param.15) | copy-start | bytes 388
  15.7 29.7 %all-to-all-start = ((bf16[16,384,128]{2,0,1:T(8,128)(2,1)}), bf16[16,384,128]{2,0,1:T(8,128)(2,1)S(1)}, u32[]{:S(2)}, u32[]{:S(2)}) async-start(bf16[16,384,128]{2,0,1:T(8,128)(2,1)} %multiply_bitcast_fusion.1), calls=%async_computation | async-start | bytes 3145728 | tf_op jit(solution)/shard_map/all_to_all | solution.py:63
  23.4 361.9 %reduce-scatter.2.cloned.1.call-start = ((), (), s32[]{:S(2)}) async-start(), calls=%async_computation.3 | async-start | bytes 2359296 | tf_op jit(solution)/shard_map/reduce_scatter | solution.py:78
  25.4 20.4 %copy-start.16 = (pred[12]{0:T(512)(128)(4,1)}, pred[12]{0:T(512)(128)(4,1)S(1)}, u32[]{:S(2)}) copy-start(pred[12]{0:T(512)(128)(4,1)S(1)} %dynamic-slice_reduce_fusion) | copy-start | bytes 40
  26.1 19.6 %copy-start.14 = (s32[12]{0:T(128)}, s32[12]{0:T(128)S(1)}, u32[]{:S(2)}) copy-start(s32[12]{0:T(128)S(1)} %select_reduce_fusion.4) | copy-start | bytes 148
  45.4 3.7 copy-start.6
  45.8 1.2 copy-start.3
  64.4 3.9 copy-start.1
  68.3 0.9 copy-start.9
  70.5 1.7 copy-start.2
  72.3 1.4 copy-start.4
  84.5 2.1 copy-start
  99.3 2.1 copy-start
  114.1 2.1 copy-start
  128.9 2.1 copy-start
  143.7 2.1 copy-start
  158.4 2.1 copy-start
  173.2 2.1 copy-start
  188.0 2.1 copy-start
  199.4 3.0 copy-start.10
  200.5 2.8 copy-start.23
  244.3 2.7 copy-start.22
  247.0 69.5 %copy-start.5 = (f32[64,12,128]{2,1,0:T(8,128)S(1)}, f32[64,12,128]{2,1,0:T(8,128)}, u32[]{:S(2)}) copy-start(f32[64,12,128]{2,1,0:T(8,128)} %copy.101) | copy-start | bytes 1179652
  247.0 69.5 %copy-start.8 = (f32[72,12,128]{2,0,1:T(8,128)S(1)}, f32[72,12,128]{2,0,1:T(8,128)}, u32[]{:S(2)}) copy-start(f32[72,12,128]{2,0,1:T(8,128)} %concatenate.18) | copy-start | bytes 1327108
  247.0 69.5 %copy-start.21 = (s32[8]{0:T(128)S(1)}, s32[8]{0:T(128)}, u32[]{:S(2)}) copy-start(s32[8]{0:T(128)} %get-tuple-element.529) | copy-start | bytes 100
  316.5 29.1 %copy-start.11 = (f32[8,12,128]{2,0,1:T(8,128)S(1)}, f32[8,12,128]{2,0,1:T(8,128)}, u32[]{:S(2)}) copy-start(f32[8,12,128]{2,0,1:T(8,128)} %get-tuple-element.130) | copy-start | bytes 147460
  345.7 0.8 copy-start.18
  345.7 0.8 copy-start.20
  348.2 6.7 %copy-start.13 = (s32[8,128]{1,0:T(8,128)S(1)}, s32[8,128]{1,0:T(8,128)}, u32[]{:S(2)}) copy-start(s32[8,128]{1,0:T(8,128)} %param.14) | copy-start | bytes 12292
  348.2 6.9 %copy-start.7 = (bf16[16,384,128]{2,0,1:T(8,128)(2,1)S(1)}, bf16[16,384,128]{2,0,1:T(8,128)(2,1)}, u32[]{:S(2)}) copy-start(bf16[16,384,128]{2,0,1:T(8,128)(2,1)} %copy-done.6) | copy-start | bytes 4718596
  348.2 34.7 %all-to-all-start.1 = ((f32[32,128,128]{2,0,1:T(8,128)}), f32[32,128,128]{2,0,1:T(8,128)}, u32[]{:S(2)}, u32[]{:S(2)}) async-start(f32[32,128,128]{2,0,1:T(8,128)} %multiply_bitcast_fusion), calls=%async_computation.1 | async-start | bytes 4194304 | tf_op jit(solution)/shard_map/all_to_all | solution.py:99
  354.8 1.3 copy-start.15
  354.8 1.3 copy-start.17
Sparse Core Ops, SparseCore 0:
  80.7 43.0 reduce-scatter.1
where the time goes:
time: 399 us; the launch traced here: 394 us
  other arithmetic  140 us (35%)
  local copies, waits for them, and re-layouts  96.4 us (24%)
  loops' own time  81.2 us (20%)
  waiting for transfers between devices  24.6 us (6%)
  blocking collectives  20 us (5%)
  between operations  14.5 us (4%)
  starting transfers between devices  14.4 us (4%)
    reduce_sum x32, other arithmetic, single_lag(): first = jnp.sum(jnp.where(valid, base, jnp.float32(0.0)), 0)  98.4 us
    another operation x4, loops' own time, multitau(): results.append(lax.map(single_lag, lag_table[level]))  81.2 us
    dynamic_slice x32, local copies, waits for them, and re-layouts, multitau(): results.append(lax.map(single_lag, lag_table[level]))  24.5 us
    reduce_sum x24, other arithmetic, single_lag(): second = jnp.sum(shifted, 0)  23.9 us
    psum x1, blocking collectives, shards(): sums = lax.psum(partial_sums, 'rows')  20 us
    all_to_all x1, waiting for transfers between devices, shards(): lax.all_to_all(packed, 'tm', split_axis=1, concat_axis=0, tiled=True)  18.1 us
    slice x6, local copies, waits for them, and re-layouts, multitau(): current = (base[0::2] + base[1::2]) * 0.5  17.8 us
    dynamic_slice x8, local copies, waits for them, and re-layouts, single_lag(): lax.dynamic_slice_in_dim(padded, lag, length, 0).astype(jnp.float32)  16 us
  transfers between devices with their start and end apart: 3, of which 2 were waited for; matrix products, arithmetic and copies ran while one was open for 49% of the time, Pallas kernels for 0%

commit v1 on v0

v1 whole, which is shorter than its diff:
```python
import functools

import jax
import jax.numpy as jnp
from jax import lax
from jax.experimental import pallas as pl
from jax.experimental.pallas import tpu as pltpu
from jax.sharding import PartitionSpec as P

CYCLES = 64
LEVELS = 4
LAGMAX = 8
MESH = pl.DeviceIdType.MESH
FLOWS = ((0, 1, 4), (1, -1, 4), (0, -1, 3), (1, 1, 3))
STEPS = 4
CODE = 14500.0
BIAS = 32767


def pack(slot_ref, x_ref, out_ref):
    out_ref[...] = jnp.zeros_like(out_ref)

    def place(b, carry):
        out_ref[slot_ref[b]] = x_ref[b]
        return carry

    lax.fori_loop(0, x_ref.shape[0], place, 0, unroll=8)


def multitau_block(b, recv_ref, pad_ref, level_ref, table_ref):
    nf = recv_ref.shape[0] * recv_ref.shape[2]
    width = recv_ref.shape[3]
    pad_ref[pl.ds(0, nf), :] = recv_ref[:, b].astype(jnp.float32).reshape(nf, width)
    sub = lax.broadcasted_iota(jnp.int32, (8, width), 0)
    for level in range(LEVELS):
        length = nf >> level
        cols = length // 8

        def get(q, level=level, cols=cols):
            if level == 0:
                return pad_ref[pl.ds(q, 8, stride=cols), :]
            return level_ref[level - 1, q]

        window = [get(q) for q in range(LAGMAX)]
        products = [None] * LAGMAX
        total = None
        heads = []
        tails = [None] * LAGMAX
        previous = None
        for q in range(cols):
            window.append(get(q + LAGMAX))
            base = window[q]
            total = base if total is None else total + base
            if q < LAGMAX:
                heads.append(base[0:1])
            if q >= cols - LAGMAX:
                tails[cols - 1 - q] = base[7:8]
            for d in range(1, LAGMAX + 1):
                term = base * window[q + d]
                products[d - 1] = term if products[d - 1] is None else products[d - 1] + term
            if level + 1 < LEVELS:
                if q % 2 == 0:
                    previous = base
                else:
                    mean = (previous + base) * 0.5
                    level_ref[level, q // 2] = mean
                    if q // 2 < LAGMAX:
                        halo = jnp.where(sub < 7, pltpu.roll(mean, 7, 0), 0.0)
                        level_ref[level, cols // 2 + q // 2] = halo
        whole = jnp.sum(total, 0, keepdims=True)
        first, second = whole, whole
        for d in range(1, LAGMAX + 1):
            first = first - tails[d - 1]
            second = second - heads[d - 1]
            product = jnp.sum(products[d - 1], 0, keepdims=True)
            denom = first * second
            safe = jnp.where(denom > 0, denom, 1.0)
            value = jnp.where(denom > 0, product * float(length - d) / safe, 0.0)
            table_ref[level * LAGMAX + d - 1, pl.ds(b, 1), :] = value


def core(
    ntm,
    nrows,
    lag_ref,
    count_ref,
    mask_ref,
    wide_ref,
    near_ref,
    g2_ref,
    two_ref,
    wide_in,
    near_in,
    pad_ref,
    level_ref,
    table_ref,
    gram_ref,
    sums_ref,
    tall_ref,
    out_buf,
    in_buf,
    local_sem,
    wide_send,
    wide_recv,
    near_send,
    near_recv,
    sum_send,
    sum_recv,
    ring_send,
    ring_recv,
):
    me = lax.axis_index("tm")
    row = lax.axis_index("rows")
    barrier = pltpu.get_barrier_semaphore()

    def hello_tm(i, carry):
        peer = lax.rem(me + i, ntm)
        pl.semaphore_signal(barrier, inc=1, device_id=(peer, row), device_id_type=MESH)
        return carry

    def hello_rows(i, carry):
        peer = lax.rem(row + i, nrows)
        pl.semaphore_signal(barrier, inc=1, device_id=(me, peer), device_id_type=MESH)
        return carry

    lax.fori_loop(1, ntm, hello_tm, 0)
    lax.fori_loop(1, nrows, hello_rows, 0)
    own_wide = pltpu.make_async_copy(wide_ref.at[me], wide_in.at[me], local_sem.at[0])
    own_near = pltpu.make_async_copy(near_ref.at[me], near_in.at[me], local_sem.at[1])
    own_wide.start()
    own_near.start()
    pad_ref[...] = jnp.zeros_like(pad_ref)
    pl.semaphore_wait(barrier, ntm + nrows - 2)

    def wide_copy(i):
        peer = lax.rem(me + i, ntm)
        return pltpu.make_async_remote_copy(
            src_ref=wide_ref.at[peer],
            dst_ref=wide_in.at[me],
            send_sem=wide_send.at[i],
            recv_sem=wide_recv.at[me],
            device_id=(peer, row),
            device_id_type=MESH,
        )

    def near_copy(i):
        peer = lax.rem(me + i, ntm)
        return pltpu.make_async_remote_copy(
            src_ref=near_ref.at[peer],
            dst_ref=near_in.at[me],
            send_sem=near_send.at[i],
            recv_sem=near_recv.at[me],
            device_id=(peer, row),
            device_id_type=MESH,
        )

    def arrival(buf, sem, i):
        peer = lax.rem(me + ntm - i, ntm)
        return pltpu.make_async_remote_copy(
            src_ref=buf.at[peer],
            dst_ref=buf.at[peer],
            send_sem=sem.at[peer],
            recv_sem=sem.at[peer],
            device_id=(peer, row),
            device_id_type=MESH,
        )

    def each(body):
        def step(i, carry):
            body(i)
            return carry

        lax.fori_loop(1, ntm, step, 0)

    each(lambda i: wide_copy(i).start())
    each(lambda i: near_copy(i).start())
    own_wide.wait()
    each(lambda i: arrival(wide_in, wide_recv, i).wait_recv())

    slots = wide_in.shape[1]
    nf = ntm * wide_in.shape[2]
    width = wide_in.shape[3]
    span = nf // nrows
    pixels = jnp.concatenate([wide_in[:, k].reshape(nf, width) for k in range(slots)], 1)
    contract = (((1,), (1,)), ((), ()))
    sums_ref[row] = lax.dot_general(
        mask_ref[...], pixels, contract, preferred_element_type=jnp.float32
    )

    def sum_copy(i):
        peer = lax.rem(row + i, nrows)
        return pltpu.make_async_remote_copy(
            src_ref=sums_ref.at[row],
            dst_ref=sums_ref.at[row],
            send_sem=sum_send.at[i],
            recv_sem=sum_recv.at[row],
            device_id=(me, peer),
            device_id_type=MESH,
        )

    def sum_arrival(i):
        peer = lax.rem(row + nrows - i, nrows)
        return pltpu.make_async_remote_copy(
            src_ref=sums_ref.at[peer],
            dst_ref=sums_ref.at[peer],
            send_sem=sum_recv.at[peer],
            recv_sem=sum_recv.at[peer],
            device_id=(me, peer),
            device_id_type=MESH,
        )

    for i in range(1, nrows):
        sum_copy(i).start()
    for a in range(2):
        gram_ref[a] = lax.dot_general(
            pixels * mask_ref[a : a + 1, :], pixels, contract, preferred_element_type=jnp.float32
        )
    for i in range(1, nrows):
        sum_arrival(i).wait_recv()
    sums = sums_ref[0]
    for i in range(1, nrows):
        sums = sums + sums_ref[i]
    tall_ref[...] = sums.T

    def own_part(a, slab):
        start = pl.multiple_of(slab * span, span)
        first = tall_ref[pl.ds(start, span), a : a + 1]
        denom = jnp.maximum(first * sums[a : a + 1, :], 1.0)
        return gram_ref[a, pl.ds(start, span), :] * (count_ref[a] / denom)

    def ring_copy(flow, step):
        _, way, hops = FLOWS[flow]
        return pltpu.make_async_remote_copy(
            src_ref=out_buf.at[flow, step],
            dst_ref=in_buf.at[flow, step],
            send_sem=ring_send.at[flow, step],
            recv_sem=ring_recv.at[flow, step],
            device_id=(me, lax.rem(row + way + nrows, nrows)),
            device_id_type=MESH,
        )

    def tau(b, carry):
        multitau_block(b, near_in, pad_ref, level_ref, table_ref)
        return carry

    for step in range(STEPS):
        for flow, (a, way, hops) in enumerate(FLOWS):
            if step >= hops:
                continue
            slab = lax.rem(row + way * (hops - step) + nrows, nrows)
            code = (own_part(a, slab) * CODE + 0.5).astype(jnp.int32)
            if step:
                ring_copy(flow, step - 1).wait_recv()
                code = code + in_buf[flow, step - 1].astype(jnp.int32)
            else:
                code = code - BIAS
            out_buf[flow, step] = code.astype(jnp.int16)
            ring_copy(flow, step).start()
        if step == 0:
            own_near.wait()
            each(lambda i: arrival(near_in, near_recv, i).wait_recv())
        lax.fori_loop(step, step + 1, tau, 0)

    for l in range(lag_ref.shape[0]):
        g2_ref[l] = table_ref[(l // LAGMAX) * LAGMAX + lag_ref[l]]
    total = [own_part(a, row) for a in range(2)]
    for flow, (a, way, hops) in enumerate(FLOWS):
        ring_copy(flow, hops - 1).wait_recv()
        code = in_buf[flow, hops - 1].astype(jnp.int32) + BIAS
        total[a] = total[a] + code.astype(jnp.float32) * (1.0 / CODE)
    for a in range(2):
        two_ref[a] = total[a]

    each(lambda i: wide_copy(i).wait_send())
    each(lambda i: near_copy(i).wait_send())
    for i in range(1, nrows):
        sum_copy(i).wait_send()
    for flow, (a, way, hops) in enumerate(FLOWS):
        for step in range(hops):
            ring_copy(flow, step).wait_send()


def shards(frames, block_owner, cycle_slot, lag_table):
    local = frames[:, 0]
    span, nblocks, width = local.shape
    ntm = lax.axis_size("tm")
    nrows = lax.axis_size("rows")
    me_tm = lax.axis_index("tm")
    me_row = lax.axis_index("rows")
    cap = 3 * nblocks // ntm
    near = nblocks // ntm
    nf = span * ntm
    owners_all = block_owner[:, :, 0]
    owners = lax.dynamic_index_in_dim(owners_all, me_row, 0, False)
    slots = lax.dynamic_index_in_dim(cycle_slot, me_row, 0, False)
    order = jnp.arange(nblocks, dtype=jnp.int32)
    rank = jnp.sum(
        ((owners[:, None] == owners[None, :]) & (order[None, :] < order[:, None])).astype(jnp.int32), 1
    )
    place = owners * cap + rank
    tall = jnp.swapaxes(local, 0, 1)
    vmem = pl.BlockSpec(memory_space=pltpu.VMEM)
    smem = pl.BlockSpec(memory_space=pltpu.SMEM)
    wide = pl.pallas_call(
        pack,
        out_shape=jax.ShapeDtypeStruct((ntm * cap, span, width), local.dtype),
        in_specs=[smem, vmem],
        out_specs=vmem,
    )(place, tall)
    lane_slot = jnp.arange(cap * width, dtype=jnp.int32) // width
    hit = (place[:, None] == me_tm * cap + lane_slot[None, :])[None] & (
        slots[None, :] == jnp.arange(8, dtype=jnp.int32)[:, None]
    )[:, :, None]
    masks = jnp.any(hit, 1).astype(jnp.bfloat16)
    cycles_all = owners_all * 2 + cycle_slot
    mine = me_tm * 2 + jnp.arange(2, dtype=jnp.int32)
    counts = width * jnp.sum((cycles_all[:, :, None] == mine).astype(jnp.float32), (0, 1))
    nflow = len(FLOWS)
    out_span = nf // nrows
    dma = pltpu.SemaphoreType.DMA
    g2, two = pl.pallas_call(
        functools.partial(core, ntm, nrows),
        out_shape=(
            jax.ShapeDtypeStruct((LEVELS * 8, near, width), jnp.float32),
            jax.ShapeDtypeStruct((2, out_span, nf), jnp.float32),
        ),
        in_specs=[smem, smem, vmem, vmem, vmem],
        out_specs=(vmem, vmem),
        scratch_shapes=[
            pltpu.VMEM((ntm, cap, span, width), jnp.bfloat16),
            pltpu.VMEM((ntm, near, span, width), jnp.bfloat16),
            pltpu.VMEM((nf + 64, width), jnp.float32),
            pltpu.VMEM((LEVELS - 1, nf // 16 + LAGMAX, 8, width), jnp.float32),
            pltpu.VMEM((LEVELS * LAGMAX, near, width), jnp.float32),
            pltpu.VMEM((2, nf, nf), jnp.float32),
            pltpu.VMEM((nrows, 8, nf), jnp.float32),
            pltpu.VMEM((nf, 8), jnp.float32),
            pltpu.VMEM((nflow, STEPS, out_span, nf), jnp.int16),
            pltpu.VMEM((nflow, STEPS, out_span, nf), jnp.int16),
            dma((2,)),
            dma((ntm,)),
            dma((ntm,)),
            dma((ntm,)),
            dma((ntm,)),
            dma((nrows,)),
            dma((nrows,)),
            dma((nflow, STEPS)),
            dma((nflow, STEPS)),
        ],
        compiler_params=pltpu.CompilerParams(collective_id=0, has_side_effects=True),
    )(
        jnp.clip(lag_table.reshape(-1) - 1, 0, LAGMAX - 1),
        counts,
        masks,
        wide.reshape(ntm, cap, span, width),
        tall.reshape(ntm, near, span, width),
    )
    return g2[None], jnp.swapaxes(two, 0, 1)


def solution(mesh):
    in_specs = (P("tm", "rows", None, None), P(), P(), P())
    out_specs = (P("rows", None, "tm", None), P("rows", "tm", None))
    return jax.shard_map(shards, mesh=mesh, in_specs=in_specs, out_specs=out_specs, check_vma=False)
```

time: 399 us -> 76 us (0.19)
  the two profiles are of different devices: /device:TPU:2 before, /device:TPU:1 now
where the time goes in v1:
time: 76 us; the launch traced here: 75.7 us
  Pallas kernels  62.9 us (83%)
  local copies, waits for them, and re-layouts  7.47 us (10%)
  other arithmetic  4.64 us (6%)
    pallas_call x1, Pallas kernels, shards(): pl.pallas_call(functools.partial(core, ntm, nrows), out_shape=(jax.ShapeD...  60.2 us
    unnamed x5, local copies, waits for them, and re-layouts  5.53 us
    pallas_call x1, Pallas kernels, shards(): pl.pallas_call(pack, out_shape=jax.ShapeDtypeStruct((ntm * cap, span, wid...  2.63 us

profile of v1, /device:TPU:1, one launch (start us, length us, event | category | flops | bytes accessed | tf_op | source)
XLA Modules:
  0.0 75.7 jit_solution(4852348958788824436)
XLA Ops:
  0.6 0.7 dynamic-slice_bitcast_fusion
  1.4 0.7 dynamic-slice_bitcast_fusion.1
  2.0 0.2 convert_reduce_fusion
  2.2 0.7 multiply_add_fusion.slot_ref
  2.9 0.0 copy-start
  2.9 0.7 add_clamp_fusion
  3.5 0.6 min.12.lag_ref
  4.1 0.7 bitcast_add_fusion
  4.8 0.2 convert_reduce_fusion.1
  5.0 0.6 broadcast_multiply_fusion.count_ref
  5.6 0.2 broadcast_compare_fusion
  5.8 0.8 %and_reduce_fusion = pred[8,1536]{1,0:T(8,128)(4,1)S(1)} fusion(pred[8,128]{1,0:T(8,128)(4,1)S(1)} %iota_compare_fusion.1, pred[128,1536]{1,0:T(8,128)(4,1)S(1)} %broadcast_compare_fusion), kind=kLoop, calls=%fused_computation | loop fusion | flops 3133440 | bytes 209920 | tf_op jit(solution)/shard_map/reduce_or | solution.py:314
  6.6 0.6 convert_element_type.11.mask_ref
  7.3 2.2 %copy.14 = bf16[16,1,128,128]{3,0,2,1:T(8,128)(2,1)} copy(bf16[16,1,128,128]{3,2,1,0:T(8,128)(2,1)} %param.4) | data formatting | bytes 1048576 | tf_op args[0]
  9.5 0.0 copy-done
  9.5 2.6 %shard_map.59 = bf16[384,16,128]{2,1,0:T(8,128)(2,1)} custom-call(s32[128]{0:T(128)} %copy-done, bf16[128,16,128]{2,1,0:T(8,128)(2,1)} %bitcast.19), custom_call_target="tpu_custom_call" | custom-call | tf_op jit(solution)/shard_map/pallas_call | solution.py:304
  12.1 60.2 %shard_map.60 = (f32[32,4,128]{2,1,0:T(4,128)}, f32[2,64,512]{2,1,0:T(8,128)}) custom-call(s32[32]{0:T(128)} %min.12.lag_ref, f32[2]{0:T(128)} %broadcast_multiply_fusion.count_ref, bf16[8,1536]{1,0:T(8,128)(2,1)} %convert_element_type.11.mask_ref, bf16[32,12,16,128]{3,2,1,0:T(8,128)(2,1)} %bitcast.18, bf16[32,4,16,128]{3,2,1,0:T(8,128)(2,1)} %bitcast.20), custom_call_target="tpu_custom_call" | custom-call | tf_op jit(solution)/shard_map/pallas_call | solution.py:321
  72.3 1.9 %copy.11 = f32[64,2,512]{2,1,0:T(2,128)} copy(f32[64,2,512]{2,0,1:T(8,128)} %bitcast.21) | data formatting | bytes 524288
  74.2 1.5 %copy.16 = f32[1,32,4,128]{3,2,1,0:T(4,128)} copy(f32[1,32,4,128]{3,2,1,0:T(4,128)} %bitcast.22) | data formatting | bytes 131072
  (3 shorter events, 0.0 us)
Async XLA Ops:
  2.9 6.6 %copy-start = (s32[128]{0:T(128)}, s32[128]{0:T(128)S(1)}, u32[]{:S(2)}) copy-start(s32[128]{0:T(128)S(1)} %multiply_add_fusion.slot_ref) | copy-start | bytes 1540

commit v2 on v1

v2 whole, which is shorter than its diff:
```python
import functools

import jax
import jax.numpy as jnp
from jax import lax
from jax.experimental import pallas as pl
from jax.experimental.pallas import tpu as pltpu
from jax.sharding import PartitionSpec as P

CYCLES = 64
LEVELS = 4
LAGMAX = 8
MESH = pl.DeviceIdType.MESH
FLOWS = ((0, 1, 4), (1, -1, 4), (0, -1, 3), (1, 1, 3))
STEPS = 4
CODE = 14500.0
BIAS = 32767


def multitau_block(b, recv_ref, pad_ref, level_ref, table_ref):
    nf = recv_ref.shape[0] * recv_ref.shape[2]
    width = recv_ref.shape[3]
    pad_ref[pl.ds(0, nf), :] = recv_ref[:, b].astype(jnp.float32).reshape(nf, width)
    sub = lax.broadcasted_iota(jnp.int32, (8, width), 0)
    for level in range(LEVELS):
        length = nf >> level
        cols = length // 8

        def get(q, level=level, cols=cols):
            if level == 0:
                return pad_ref[pl.ds(q, 8, stride=cols), :]
            return level_ref[level - 1, q]

        window = [get(q) for q in range(LAGMAX)]
        products = [None] * LAGMAX
        total = None
        heads = []
        tails = [None] * LAGMAX
        previous = None
        for q in range(cols):
            window.append(get(q + LAGMAX))
            base = window[q]
            total = base if total is None else total + base
            if q < LAGMAX:
                heads.append(base[0:1])
            if q >= cols - LAGMAX:
                tails[cols - 1 - q] = base[7:8]
            for d in range(1, LAGMAX + 1):
                term = base * window[q + d]
                products[d - 1] = term if products[d - 1] is None else products[d - 1] + term
            if level + 1 < LEVELS:
                if q % 2 == 0:
                    previous = base
                else:
                    mean = (previous + base) * 0.5
                    level_ref[level, q // 2] = mean
                    if q // 2 < LAGMAX:
                        halo = jnp.where(sub < 7, pltpu.roll(mean, 7, 0), 0.0)
                        level_ref[level, cols // 2 + q // 2] = halo
        whole = jnp.sum(total, 0, keepdims=True)
        first, second = whole, whole
        for d in range(1, LAGMAX + 1):
            first = first - tails[d - 1]
            second = second - heads[d - 1]
            product = jnp.sum(products[d - 1], 0, keepdims=True)
            denom = first * second
            safe = jnp.where(denom > 0, denom, 1.0)
            value = jnp.where(denom > 0, product * float(length - d) / safe, 0.0)
            table_ref[level * LAGMAX + d - 1, pl.ds(b, 1), :] = value


def far_first(ny, nx):
    offsets = [(dy, dx, dc) for dy in range(ny) for dx in range(nx) for dc in range(2)][1:]
    return sorted(offsets, key=lambda o: -(min(o[0], ny - o[0]) + min(o[1], nx - o[1])))


def core(
    ntm,
    nrows,
    lag_ref,
    owner_ref,
    slot_ref,
    frames_ref,
    g2_ref,
    two_ref,
    raw,
    flat,
    near_out,
    wide_out,
    wide_in,
    near_in,
    table_vec,
    table,
    pad_ref,
    level_ref,
    corr_ref,
    gram_ref,
    sums_ref,
    tall_ref,
    out_buf,
    in_buf,
    local_sem,
    wide_send,
    wide_recv,
    near_send,
    near_recv,
    sum_send,
    sum_recv,
    ring_send,
    ring_recv,
):
    me = lax.axis_index("tm")
    row = lax.axis_index("rows")
    nx = 4
    ny = ntm // (2 * nx)
    barrier = pltpu.get_barrier_semaphore()
    load = pltpu.make_async_copy(frames_ref.at[:, 0], raw, local_sem.at[0])
    load.start()

    def hello_tm(i, carry):
        peer = lax.rem(me + i, ntm)
        pl.semaphore_signal(barrier, inc=1, device_id=(peer, row), device_id_type=MESH)
        return carry

    def hello_rows(i, carry):
        peer = lax.rem(row + i, nrows)
        pl.semaphore_signal(barrier, inc=1, device_id=(me, peer), device_id_type=MESH)
        return carry

    lax.fori_loop(1, ntm, hello_tm, 0)
    lax.fori_loop(1, nrows, hello_rows, 0)

    span, nblocks, width = raw.shape
    slots = wide_in.shape[1]
    near = near_in.shape[1]
    square = (nblocks, nblocks)
    owners = owner_ref[pl.ds(row, 1), :].astype(jnp.float32)
    cycles = slot_ref[pl.ds(row, 1), :].astype(jnp.float32)
    down = lax.broadcasted_iota(jnp.int32, square, 0)
    along = lax.broadcasted_iota(jnp.int32, square, 1)
    alongf = along.astype(jnp.float32)
    across = jnp.broadcast_to(owners, square)
    same = (across == across.T) & (down < along)
    rank = jnp.sum(jnp.where(same, 1.0, 0.0), 0, keepdims=True)
    place = jnp.broadcast_to(owners * float(slots) + rank, square).T
    entry = jnp.broadcast_to(alongf[0:1] + float(nblocks) * (1.0 + cycles), square).T
    parts = ntm * slots // nblocks
    rows_of = [
        jnp.sum(jnp.where(place == alongf + float(j * nblocks), entry, 0.0), 0, keepdims=True)
        for j in range(parts)
    ]
    table_vec[...] = jnp.concatenate(
        rows_of + [jnp.zeros((8 - parts, nblocks), jnp.float32)], 0
    ).astype(jnp.int32)
    fetch = pltpu.make_async_copy(table_vec, table, local_sem.at[1])
    fetch.start()
    pad_ref[...] = jnp.zeros_like(pad_ref)
    load.wait()
    flat[...] = raw[...].astype(jnp.float32).reshape(span * nblocks, width)

    def turn(b, carry):
        near_out[b // near, b % near] = flat[pl.ds(b, span, stride=nblocks), :].astype(jnp.bfloat16)
        return carry

    lax.fori_loop(0, nblocks, turn, 0, unroll=8)
    fetch.wait()

    def entry_at(i):
        return table[i // nblocks, i % nblocks]

    def fill(o, carry):
        for k in range(slots):
            b = entry_at(o * slots + k) % nblocks
            wide_out[o, k] = near_out[b // near, b % near]
        return carry

    lax.fori_loop(0, ntm, fill, 0)
    wide_in[me] = wide_out[me]
    near_in[me] = near_out[me]
    pl.semaphore_wait(barrier, ntm + nrows - 2)

    order = far_first(ny, nx)
    y, x, c = me // (2 * nx), (me // 2) % nx, me % 2

    def peer_at(offset):
        dy, dx, dc = offset
        return (lax.rem(y + dy, ny) * nx + lax.rem(x + dx, nx)) * 2 + lax.rem(c + dc, 2)

    def plane_copy(out, into, send, recv, peer):
        return pltpu.make_async_remote_copy(
            src_ref=out.at[peer],
            dst_ref=into.at[me],
            send_sem=send.at[peer],
            recv_sem=recv.at[me],
            device_id=(peer, row),
            device_id_type=MESH,
        )

    def wide_copy(peer):
        return plane_copy(wide_out, wide_in, wide_send, wide_recv, peer)

    def near_copy(peer):
        return plane_copy(near_out, near_in, near_send, near_recv, peer)

    def arrival(buf, sem, peer):
        return pltpu.make_async_remote_copy(
            src_ref=buf.at[peer],
            dst_ref=buf.at[peer],
            send_sem=sem.at[peer],
            recv_sem=sem.at[peer],
            device_id=(peer, row),
            device_id_type=MESH,
        )

    def each(body):
        def step(i, carry):
            body(lax.rem(me + i, ntm))
            return carry

        lax.fori_loop(1, ntm, step, 0)

    for offset in order:
        wide_copy(peer_at(offset)).start()
    for offset in order:
        near_copy(peer_at(offset)).start()
    each(lambda peer: arrival(wide_in, wide_recv, peer).wait_recv())

    nf = ntm * span
    slab_len = nf // nrows
    pixels = [wide_in[:, k].reshape(nf, width) for k in range(slots)]
    whole = jnp.concatenate(pixels, 1)
    own_entries = [entry_at(me * slots + k) // nblocks for k in range(slots)]
    flags = [
        [jnp.where(e == a + 1, 1.0, 0.0) for e in own_entries] for a in range(2)
    ]
    contract = (((1,), (1,)), ((), ()))
    lines = [
        jnp.concatenate([jnp.full((1, width), f, jnp.float32) for f in flags[a]], 1) for a in range(2)
    ]
    masks = jnp.concatenate(lines + [jnp.zeros((6, slots * width), jnp.float32)], 0)
    masks = masks.astype(jnp.bfloat16)
    sums_ref[row] = lax.dot_general(masks, whole, contract, preferred_element_type=jnp.float32)

    def sum_copy(i):
        peer = lax.rem(row + i, nrows)
        return pltpu.make_async_remote_copy(
            src_ref=sums_ref.at[row],
            dst_ref=sums_ref.at[row],
            send_sem=sum_send.at[i],
            recv_sem=sum_recv.at[row],
            device_id=(me, peer),
            device_id_type=MESH,
        )

    def sum_arrival(i):
        peer = lax.rem(row + nrows - i, nrows)
        return pltpu.make_async_remote_copy(
            src_ref=sums_ref.at[peer],
            dst_ref=sums_ref.at[peer],
            send_sem=sum_recv.at[peer],
            recv_sem=sum_recv.at[peer],
            device_id=(me, peer),
            device_id_type=MESH,
        )

    for i in range(1, nrows):
        sum_copy(i).start()
    for a in range(2):
        gram_ref[a] = lax.dot_general(
            whole * masks[a : a + 1, :], whole, contract, preferred_element_type=jnp.float32
        )
    cycle_all = owner_ref[...] * 2 + slot_ref[...]
    counts = []
    for a in range(2):
        hits = jnp.where(cycle_all == me * 2 + a, float(width), 0.0)
        counts.append(jnp.sum(jnp.sum(hits, 1, keepdims=True), 0, keepdims=True))
    for i in range(1, nrows):
        sum_arrival(i).wait_recv()
    sums = sums_ref[0]
    for i in range(1, nrows):
        sums = sums + sums_ref[i]
    tall_ref[...] = sums.T

    def own_part(a, slab):
        start = pl.multiple_of(slab * slab_len, slab_len)
        first = tall_ref[pl.ds(start, slab_len), a : a + 1]
        denom = jnp.maximum(first * sums[a : a + 1, :], 1.0)
        return gram_ref[a, pl.ds(start, slab_len), :] * (counts[a] / denom)

    def ring_copy(flow, step):
        _, way, hops = FLOWS[flow]
        return pltpu.make_async_remote_copy(
            src_ref=out_buf.at[flow, step],
            dst_ref=in_buf.at[flow, step],
            send_sem=ring_send.at[flow, step],
            recv_sem=ring_recv.at[flow, step],
            device_id=(me, lax.rem(row + way + nrows, nrows)),
            device_id_type=MESH,
        )

    def tau(b, carry):
        multitau_block(b, near_in, pad_ref, level_ref, corr_ref)
        return carry

    for step in range(STEPS):
        for flow, (a, way, hops) in enumerate(FLOWS):
            if step >= hops:
                continue
            slab = lax.rem(row + way * (hops - step) + nrows, nrows)
            code = (own_part(a, slab) * CODE + 0.5).astype(jnp.int32)
            if step:
                ring_copy(flow, step - 1).wait_recv()
                code = code + in_buf[flow, step - 1].astype(jnp.int32)
            else:
                code = code - BIAS
            out_buf[flow, step] = code.astype(jnp.int16)
            ring_copy(flow, step).start()
        if step == 1:
            each(lambda peer: arrival(near_in, near_recv, peer).wait_recv())
        if step >= 1:
            lax.fori_loop((0, 0, 1, 2)[step], (0, 1, 2, 4)[step], tau, 0)

    for l in range(LEVELS):
        for j in range(lag_ref.shape[1]):
            g2_ref[l * lag_ref.shape[1] + j] = corr_ref[
                l * LAGMAX + jnp.maximum(lag_ref[l, j] - 1, 0)
            ]
    total = [own_part(a, row) for a in range(2)]
    for flow, (a, way, hops) in enumerate(FLOWS):
        ring_copy(flow, hops - 1).wait_recv()
        code = in_buf[flow, hops - 1].astype(jnp.int32) + BIAS
        total[a] = total[a] + code.astype(jnp.float32) * (1.0 / CODE)
    for a in range(2):
        two_ref[a] = total[a]

    each(lambda peer: wide_copy(peer).wait_send())
    each(lambda peer: near_copy(peer).wait_send())
    for i in range(1, nrows):
        sum_copy(i).wait_send()
    for flow, (a, way, hops) in enumerate(FLOWS):
        for step in range(hops):
            ring_copy(flow, step).wait_send()


def shards(frames, block_owner, cycle_slot, lag_table):
    span, _, nblocks, width = frames.shape
    ntm = lax.axis_size("tm")
    nrows = lax.axis_size("rows")
    cap = 3 * nblocks // ntm
    near = nblocks // ntm
    nf = span * ntm
    slab = nf // nrows
    nflow = len(FLOWS)
    vmem = pl.BlockSpec(memory_space=pltpu.VMEM)
    smem = pl.BlockSpec(memory_space=pltpu.SMEM)
    dma = pltpu.SemaphoreType.DMA
    bf16, f32, i32, i16 = jnp.bfloat16, jnp.float32, jnp.int32, jnp.int16
    g2, two = pl.pallas_call(
        functools.partial(core, ntm, nrows),
        out_shape=(
            jax.ShapeDtypeStruct((LEVELS * lag_table.shape[1], near, width), f32),
            jax.ShapeDtypeStruct((2, slab, nf), f32),
        ),
        in_specs=[smem, vmem, vmem, pl.BlockSpec(memory_space=pl.ANY)],
        out_specs=(vmem, vmem),
        scratch_shapes=[
            pltpu.VMEM((span, nblocks, width), bf16),
            pltpu.VMEM((span * nblocks, width), f32),
            pltpu.VMEM((ntm, near, span, width), bf16),
            pltpu.VMEM((ntm, cap, span, width), bf16),
            pltpu.VMEM((ntm, cap, span, width), bf16),
            pltpu.VMEM((ntm, near, span, width), bf16),
            pltpu.VMEM((8, nblocks), i32),
            pltpu.SMEM((8, nblocks), i32),
            pltpu.VMEM((nf + 64, width), f32),
            pltpu.VMEM((LEVELS - 1, nf // 16 + LAGMAX, 8, width), f32),
            pltpu.VMEM((LEVELS * LAGMAX, near, width), f32),
            pltpu.VMEM((2, nf, nf), f32),
            pltpu.VMEM((nrows, 8, nf), f32),
            pltpu.VMEM((nf, 8), f32),
            pltpu.VMEM((nflow, STEPS, slab, nf), i16),
            pltpu.VMEM((nflow, STEPS, slab, nf), i16),
            dma((2,)),
            dma((ntm,)),
            dma((ntm,)),
            dma((ntm,)),
            dma((ntm,)),
            dma((nrows,)),
            dma((nrows,)),
            dma((nflow, STEPS)),
            dma((nflow, STEPS)),
        ],
        compiler_params=pltpu.CompilerParams(collective_id=0, has_side_effects=True),
    )(lag_table, block_owner[:, :, 0], cycle_slot, frames)
    return g2[None], jnp.swapaxes(two, 0, 1)


def solution(mesh):
    in_specs = (P("tm", "rows", None, None), P(), P(), P())
    out_specs = (P("rows", None, "tm", None), P("rows", "tm", None))
    return jax.shard_map(shards, mesh=mesh, in_specs=in_specs, out_specs=out_specs, check_vma=False)
```

time: 76 us -> 64 us (0.84)
  the two profiles are of different devices: /device:TPU:1 before, /device:TPU:2 now
where the time goes in v2:
time: 64 us; the launch traced here: 63.7 us
  Pallas kernels  60.5 us (95%)
  local copies, waits for them, and re-layouts  2.52 us (4%)
  between operations  0.65 us (1%)
    pallas_call x1, Pallas kernels, shards(): pl.pallas_call(functools.partial(core, ntm, nrows), out_shape=(jax.ShapeD...  60.5 us
    unnamed x4, local copies, waits for them, and re-layouts  2.52 us

profile of v2, /device:TPU:2, one launch (start us, length us, event | category | flops | bytes accessed | tf_op | source)
XLA Modules:
  0.0 63.7 jit_solution(11384722918614332574)
XLA Ops:
  0.6 60.5 %shard_map.59 = (f32[32,4,128]{2,1,0:T(4,128)}, f32[2,64,512]{2,1,0:T(8,128)}) custom-call(s32[4,8]{1,0:T(4,128)} %lag_ref.1, s32[8,128]{1,0:T(8,128)} %bitcast.5, s32[8,128]{1,0:T(8,128)} %slot_ref.1, bf16[16,1,128,128]{3,2,1,0:T(8,128)(2,1)} %frames_ref.1), custom_call_target="tpu_custom_call" | custom-call | tf_op jit(solution)/shard_map/pallas_call | solution.py:358
  61.2 0.0 copy-start
  61.2 1.9 %copy.6 = f32[64,2,512]{2,1,0:T(2,128)} copy(f32[64,2,512]{2,0,1:T(8,128)} %bitcast.3) | data formatting | bytes 524288
  63.1 0.0 copy-done
  63.1 0.6 copy.8
Async XLA Ops:
  61.2 1.9 %copy-start = (f32[32,4,128]{2,1,0:T(4,128)S(1)}, f32[32,4,128]{2,1,0:T(4,128)}, u32[]{:S(2)}) copy-start(f32[32,4,128]{2,1,0:T(4,128)} %get-tuple-element.4) | copy-start | bytes 196612

commit v3 on v2

--- a/solution.py
+++ b/solution.py
@@ -131,7 +131,9 @@
     lax.fori_loop(1, nrows, hello_rows, 0)
 
     span, nblocks, width = raw.shape
-    slots = wide_in.shape[1]
+    halves, _, half = wide_in.shape[:3]
+    slots = halves * half
+    pitch = 16
     near = near_in.shape[1]
     square = (nblocks, nblocks)
     owners = owner_ref[pl.ds(row, 1), :].astype(jnp.float32)
@@ -142,9 +144,9 @@
     across = jnp.broadcast_to(owners, square)
     same = (across == across.T) & (down < along)
     rank = jnp.sum(jnp.where(same, 1.0, 0.0), 0, keepdims=True)
-    place = jnp.broadcast_to(owners * float(slots) + rank, square).T
+    place = jnp.broadcast_to(owners * float(pitch) + rank, square).T
     entry = jnp.broadcast_to(alongf[0:1] + float(nblocks) * (1.0 + cycles), square).T
-    parts = ntm * slots // nblocks
+    parts = ntm * pitch // nblocks
     rows_of = [
         jnp.sum(jnp.where(place == alongf + float(j * nblocks), entry, 0.0), 0, keepdims=True)
         for j in range(parts)
@@ -159,24 +161,27 @@
     flat[...] = raw[...].astype(jnp.float32).reshape(span * nblocks, width)
 
     def turn(b, carry):
-        near_out[b // near, b % near] = flat[pl.ds(b, span, stride=nblocks), :].astype(jnp.bfloat16)
+        near_out[b] = flat[pl.ds(b, span, stride=nblocks), :].astype(jnp.bfloat16)
         return carry
 
     lax.fori_loop(0, nblocks, turn, 0, unroll=8)
     fetch.wait()
 
-    def entry_at(i):
-        return table[i // nblocks, i % nblocks]
+    per = nblocks // pitch
+
+    def entry_at(owner, k):
+        return table[owner // per, (owner % per) * pitch + k]
 
     def fill(o, carry):
+        tiles = [near_out[entry_at(o, k) & (nblocks - 1)] for k in range(slots)]
         for k in range(slots):
-            b = entry_at(o * slots + k) % nblocks
-            wide_out[o, k] = near_out[b // near, b % near]
+            wide_out[k // half, o, k % half] = tiles[k]
         return carry
 
     lax.fori_loop(0, ntm, fill, 0)
-    wide_in[me] = wide_out[me]
-    near_in[me] = near_out[me]
+    for h in range(halves):
+        wide_in[h, me] = wide_out[h, me]
+    near_in[me] = near_out[pl.ds(pl.multiple_of(me * near, near), near)]
     pl.semaphore_wait(barrier, ntm + nrows - 2)
 
     order = far_first(ny, nx)
@@ -186,31 +191,38 @@
         dy, dx, dc = offset
         return (lax.rem(y + dy, ny) * nx + lax.rem(x + dx, nx)) * 2 + lax.rem(c + dc, 2)
 
-    def plane_copy(out, into, send, recv, peer):
-        return pltpu.make_async_remote_copy(
-            src_ref=out.at[peer],
-            dst_ref=into.at[me],
-            send_sem=send.at[peer],
-            recv_sem=recv.at[me],
+    def wide_copy(h, peer):
+        return pltpu.make_async_remote_copy(
+            src_ref=wide_out.at[h, peer],
+            dst_ref=wide_in.at[h, me],
+            send_sem=wide_send.at[h, peer],
+            recv_sem=wide_recv.at[h, me],
             device_id=(peer, row),
             device_id_type=MESH,
         )
 
-    def wide_copy(peer):
-        return plane_copy(wide_out, wide_in, wide_send, wide_recv, peer)
-
     def near_copy(peer):
-        return plane_copy(near_out, near_in, near_send, near_recv, peer)
-
-    def arrival(buf, sem, peer):
-        return pltpu.make_async_remote_copy(
-            src_ref=buf.at[peer],
-            dst_ref=buf.at[peer],
-            send_sem=sem.at[peer],
-            recv_sem=sem.at[peer],
+        return pltpu.make_async_remote_copy(
+            src_ref=near_out.at[pl.ds(pl.multiple_of(peer * near, near), near)],
+            dst_ref=near_in.at[me],
+            send_sem=near_send.at[peer],
+            recv_sem=near_recv.at[me],
             device_id=(peer, row),
             device_id_type=MESH,
         )
+
+    def arrival(ref, sem, peer):
+        return pltpu.make_async_remote_copy(
+            src_ref=ref,
+            dst_ref=ref,
+            send_sem=sem,
+            recv_sem=sem,
+            device_id=(peer, row),
+            device_id_type=MESH,
+        )
+
+    def wide_arrival(h, peer):
+        return arrival(wide_in.at[h, peer], wide_recv.at[h, peer], peer)
 
     def each(body):
         def step(i, carry):
@@ -218,28 +230,6 @@
             return carry
 
         lax.fori_loop(1, ntm, step, 0)
-
-    for offset in order:
-        wide_copy(peer_at(offset)).start()
-    for offset in order:
-        near_copy(peer_at(offset)).start()
-    each(lambda peer: arrival(wide_in, wide_recv, peer).wait_recv())
-
-    nf = ntm * span
-    slab_len = nf // nrows
-    pixels = [wide_in[:, k].reshape(nf, width) for k in range(slots)]
-    whole = jnp.concatenate(pixels, 1)
-    own_entries = [entry_at(me * slots + k) // nblocks for k in range(slots)]
-    flags = [
-        [jnp.where(e == a + 1, 1.0, 0.0) for e in own_entries] for a in range(2)
-    ]
-    contract = (((1,), (1,)), ((), ()))
-    lines = [
-        jnp.concatenate([jnp.full((1, width), f, jnp.float32) for f in flags[a]], 1) for a in range(2)
-    ]
-    masks = jnp.concatenate(lines + [jnp.zeros((6, slots * width), jnp.float32)], 0)
-    masks = masks.astype(jnp.bfloat16)
-    sums_ref[row] = lax.dot_general(masks, whole, contract, preferred_element_type=jnp.float32)
 
     def sum_copy(i):
         peer = lax.rem(row + i, nrows)
@@ -253,7 +243,7 @@
         )
 
     def sum_arrival(i):
-        peer = lax.rem(row + nrows - i, nrows)
+        peer = lax.rem(row + i, nrows)
         return pltpu.make_async_remote_copy(
             src_ref=sums_ref.at[peer],
             dst_ref=sums_ref.at[peer],
@@ -263,29 +253,72 @@
             device_id_type=MESH,
         )
 
-    for i in range(1, nrows):
-        sum_copy(i).start()
-    for a in range(2):
-        gram_ref[a] = lax.dot_general(
-            whole * masks[a : a + 1, :], whole, contract, preferred_element_type=jnp.float32
-        )
+    for h in range(halves):
+        for offset in order:
+            wide_copy(h, peer_at(offset)).start()
+    for offset in order:
+        near_copy(peer_at(offset)).start()
+
+    nf = ntm * span
+    slab_len = nf // nrows
+    contract = (((1,), (1,)), ((), ()))
+    own_entries = [entry_at(me, k) // nblocks for k in range(slots)]
+    sums_own = None
+    for h in range(halves):
+        lines = [
+            jnp.concatenate(
+                [
+                    jnp.full((1, width), jnp.where(e == a + 1, 1.0, 0.0), jnp.float32)
+                    for e in own_entries[h * half : (h + 1) * half]
+                ],
+                1,
+            )
+            for a in range(2)
+        ]
+        masks = jnp.concatenate(lines + [jnp.zeros((6, half * width), jnp.float32)], 0)
+        masks = masks.astype(jnp.bfloat16)
+        each(lambda peer: wide_arrival(h, peer).wait_recv())
+        pixels = jnp.concatenate([wide_in[h, :, k].reshape(nf, width) for k in range(half)], 1)
+        term = lax.dot_general(masks, pixels, contract, preferred_element_type=jnp.float32)
+        sums_own = term if sums_own is None else sums_own + term
+        if h + 1 == halves:
+            sums_own = sums_own[0:2]
+            sums_ref[row] = sums_own
+            for i in range(1, nrows):
+                sum_copy(i).start()
+        for a in range(2):
+            part = lax.dot_general(
+                pixels * masks[a : a + 1, :], pixels, contract, preferred_element_type=jnp.float32
+            )
+            if h:
+                gram_ref[a] += part
+            else:
+                gram_ref[a] = part
+
     cycle_all = owner_ref[...] * 2 + slot_ref[...]
-    counts = []
-    for a in range(2):
-        hits = jnp.where(cycle_all == me * 2 + a, float(width), 0.0)
-        counts.append(jnp.sum(jnp.sum(hits, 1, keepdims=True), 0, keepdims=True))
-    for i in range(1, nrows):
-        sum_arrival(i).wait_recv()
-    sums = sums_ref[0]
-    for i in range(1, nrows):
-        sums = sums + sums_ref[i]
-    tall_ref[...] = sums.T
+    group = lax.broadcasted_iota(jnp.int32, (nrows, 1), 0)
+    behind = lax.rem(row - group + nrows, nrows)
+    ahead = lax.rem(group - row + nrows, nrows)
+    pixel_counts = [
+        jnp.sum(jnp.where(cycle_all == me * 2 + a, float(width), 0.0), 1, keepdims=True) for a in range(2)
+    ]
+
+    def count_of(a, inside):
+        return jnp.sum(jnp.where(inside, pixel_counts[a], 0.0), 0, keepdims=True)
+
+    def inverse(v):
+        return jnp.where(v > 0, 1.0 / jnp.where(v > 0, v, 1.0), 0.0)
+
+    def sums_at(i):
+        return sums_ref[lax.rem(row + i, nrows)]
+
+    def tall_at(slab, lane):
+        start = pl.multiple_of(slab * slab_len, slab_len)
+        return tall_ref[pl.ds(start, slab_len), lane : lane + 1]
 
     def own_part(a, slab):
         start = pl.multiple_of(slab * slab_len, slab_len)
-        first = tall_ref[pl.ds(start, slab_len), a : a + 1]
-        denom = jnp.maximum(first * sums[a : a + 1, :], 1.0)
-        return gram_ref[a, pl.ds(start, slab_len), :] * (counts[a] / denom)
+        return gram_ref[a, pl.ds(start, slab_len), :]
 
     def ring_copy(flow, step):
         _, way, hops = FLOWS[flow]
@@ -302,38 +335,64 @@
         multitau_block(b, near_in, pad_ref, level_ref, corr_ref)
         return carry
 
+    def decode(flow, step, slab, lane, line):
+        a, way, _ = FLOWS[flow]
+        distance = behind if way > 0 else ahead
+        count = count_of(a, (distance >= 1) & (distance <= step))
+        value = (in_buf[flow, step - 1].astype(jnp.int32) + BIAS).astype(jnp.float32)
+        return value * (tall_at(slab, lane) * (inverse(count) * (1.0 / CODE))) * line
+
+    up = jnp.zeros_like(sums_own)
+    dn = jnp.zeros_like(sums_own)
     for step in range(STEPS):
+        if step:
+            sum_arrival(step).wait_recv()
+            sum_arrival(nrows - step).wait_recv()
+            up = up + sums_at(nrows - step)
+            dn = dn + sums_at(step)
+        lines = jnp.concatenate([up, dn, inverse(up + sums_own), inverse(dn + sums_own)], 0)
+        tall_ref[...] = lines.T
         for flow, (a, way, hops) in enumerate(FLOWS):
             if step >= hops:
                 continue
             slab = lax.rem(row + way * (hops - step) + nrows, nrows)
-            code = (own_part(a, slab) * CODE + 0.5).astype(jnp.int32)
+            lane = a if way > 0 else 2 + a
+            value = own_part(a, slab)
             if step:
                 ring_copy(flow, step - 1).wait_recv()
-                code = code + in_buf[flow, step - 1].astype(jnp.int32)
-            else:
-                code = code - BIAS
+                value = value + decode(flow, step, slab, lane, lines[lane : lane + 1])
+            count = count_of(a, (behind if way > 0 else ahead) <= step)
+            scale = tall_at(slab, lane + 4) * (count * CODE)
+            code = (value * scale * lines[lane + 4 : lane + 5] + 0.5).astype(jnp.int32) - BIAS
             out_buf[flow, step] = code.astype(jnp.int16)
             ring_copy(flow, step).start()
-        if step == 1:
-            each(lambda peer: arrival(near_in, near_recv, peer).wait_recv())
-        if step >= 1:
-            lax.fori_loop((0, 0, 1, 2)[step], (0, 1, 2, 4)[step], tau, 0)
+        if step == 2:
+            each(lambda peer: arrival(near_in.at[peer], near_recv.at[peer], peer).wait_recv())
+        if step >= 2:
+            lax.fori_loop(2 * step - 4, 2 * step - 2, tau, 0)
 
     for l in range(LEVELS):
         for j in range(lag_ref.shape[1]):
             g2_ref[l * lag_ref.shape[1] + j] = corr_ref[
                 l * LAGMAX + jnp.maximum(lag_ref[l, j] - 1, 0)
             ]
+    sum_arrival(STEPS).wait_recv()
+    last = sums_at(STEPS)
+    sums = sums_own + up + dn + last
+    ends = [up[0:1] + last[0:1], up[1:2], dn[0:1], dn[1:2] + last[1:2]]
+    lines = jnp.concatenate(ends + [sums, sums], 0)
+    tall_ref[...] = lines.T
     total = [own_part(a, row) for a in range(2)]
     for flow, (a, way, hops) in enumerate(FLOWS):
         ring_copy(flow, hops - 1).wait_recv()
-        code = in_buf[flow, hops - 1].astype(jnp.int32) + BIAS
-        total[a] = total[a] + code.astype(jnp.float32) * (1.0 / CODE)
+        lane = a if way > 0 else 2 + a
+        total[a] = total[a] + decode(flow, hops, row, lane, lines[lane : lane + 1])
     for a in range(2):
-        two_ref[a] = total[a]
-
-    each(lambda peer: wide_copy(peer).wait_send())
+        denom = jnp.maximum(tall_at(row, 4 + a) * sums[a : a + 1], 1.0)
+        two_ref[:, a, :] = total[a] * (count_of(a, behind >= 0) / denom)
+
+    for h in range(halves):
+        each(lambda peer: wide_copy(h, peer).wait_send())
     each(lambda peer: near_copy(peer).wait_send())
     for i in range(1, nrows):
         sum_copy(i).wait_send()
@@ -359,16 +418,16 @@
         functools.partial(core, ntm, nrows),
         out_shape=(
             jax.ShapeDtypeStruct((LEVELS * lag_table.shape[1], near, width), f32),
-            jax.ShapeDtypeStruct((2, slab, nf), f32),
+            jax.ShapeDtypeStruct((slab, 2, nf), f32),
         ),
         in_specs=[smem, vmem, vmem, pl.BlockSpec(memory_space=pl.ANY)],
         out_specs=(vmem, vmem),
         scratch_shapes=[
             pltpu.VMEM((span, nblocks, width), bf16),
             pltpu.VMEM((span * nblocks, width), f32),
-            pltpu.VMEM((ntm, near, span, width), bf16),
-            pltpu.VMEM((ntm, cap, span, width), bf16),
-            pltpu.VMEM((ntm, cap, span, width), bf16),
+            pltpu.VMEM((nblocks, span, width), bf16),
+            pltpu.VMEM((2, ntm, cap // 2, span, width), bf16),
+            pltpu.VMEM((2, ntm, cap // 2, span, width), bf16),
             pltpu.VMEM((ntm, near, span, width), bf16),
             pltpu.VMEM((8, nblocks), i32),
             pltpu.SMEM((8, nblocks), i32),
@@ -376,13 +435,13 @@
             pltpu.VMEM((LEVELS - 1, nf // 16 + LAGMAX, 8, width), f32),
             pltpu.VMEM((LEVELS * LAGMAX, near, width), f32),
             pltpu.VMEM((2, nf, nf), f32),
-            pltpu.VMEM((nrows, 8, nf), f32),
+            pltpu.VMEM((nrows, 2, nf), f32),
             pltpu.VMEM((nf, 8), f32),
             pltpu.VMEM((nflow, STEPS, slab, nf), i16),
             pltpu.VMEM((nflow, STEPS, slab, nf), i16),
             dma((2,)),
-            dma((ntm,)),
-            dma((ntm,)),
+            dma((2, ntm)),
+            dma((2, ntm)),
             dma((ntm,)),
             dma((ntm,)),
             dma((nrows,)),
@@ -392,7 +451,7 @@
         ],
         compiler_params=pltpu.CompilerParams(collective_id=0, has_side_effects=True),
     )(lag_table, block_owner[:, :, 0], cycle_slot, frames)
-    return g2[None], jnp.swapaxes(two, 0, 1)
+    return g2[None], two
 
 
 def solution(mesh):

time: 64 us -> 57.3 us (0.90)
  the two profiles are of different devices: /device:TPU:2 before, /device:TPU:5 now
where the time goes in v3:
time: 57.3 us; the launch traced here: 57.1 us
  Pallas kernels  53.3 us (93%)
  local copies, waits for them, and re-layouts  3.14 us (5%)
  between operations  0.64 us (1%)
    pallas_call x1, Pallas kernels, shards(): pl.pallas_call(functools.partial(core, ntm, nrows), out_shape=(jax.ShapeD...  53.3 us
    unnamed x2, local copies, waits for them, and re-layouts  3.14 us

profile of v3, /device:TPU:5, one launch (start us, length us, event | category | flops | bytes accessed | tf_op | source)
XLA Modules:
  0.0 57.1 jit_solution(5305162030048001445)
XLA Ops:
  0.6 53.3 %shard_map.59 = (f32[32,4,128]{2,1,0:T(4,128)}, f32[64,2,512]{2,1,0:T(2,128)}) custom-call(s32[4,8]{1,0:T(4,128)} %lag_ref.1, s32[8,128]{1,0:T(8,128)} %bitcast.3, s32[8,128]{1,0:T(8,128)} %slot_ref.1, bf16[16,1,128,128]{3,2,1,0:T(8,128)(2,1)} %frames_ref.1), custom_call_target="tpu_custom_call" | custom-call | tf_op jit(solution)/shard_map/pallas_call | solution.py:417
  53.9 1.5 %copy.8 = f32[1,32,4,128]{3,2,1,0:T(4,128)} copy(f32[1,32,4,128]{3,2,1,0:T(4,128)} %bitcast.2) | data formatting | bytes 131072
  55.4 1.7 %copy.9 = f32[64,2,512]{2,1,0:T(2,128)} copy(f32[64,2,512]{2,1,0:T(2,128)} %get-tuple-element.9) | data formatting | bytes 524288

commit v4 on v3

--- a/solution.py
+++ b/solution.py
@@ -71,7 +71,12 @@
 
 def far_first(ny, nx):
     offsets = [(dy, dx, dc) for dy in range(ny) for dx in range(nx) for dc in range(2)][1:]
-    return sorted(offsets, key=lambda o: -(min(o[0], ny - o[0]) + min(o[1], nx - o[1])))
+    order = []
+    for dy, dx, dc in sorted(offsets, key=lambda o: -(min(o[0], ny - o[0]) + min(o[1], nx - o[1]))):
+        for offset in ((dy, dx, dc), (-dy % ny, -dx % nx, dc)):
+            if offset not in order:
+                order.append(offset)
+    return order
 
 
 def core(
@@ -117,18 +122,12 @@
     load = pltpu.make_async_copy(frames_ref.at[:, 0], raw, local_sem.at[0])
     load.start()
 
-    def hello_tm(i, carry):
+    for i in range(1, ntm):
         peer = lax.rem(me + i, ntm)
         pl.semaphore_signal(barrier, inc=1, device_id=(peer, row), device_id_type=MESH)
-        return carry
-
-    def hello_rows(i, carry):
+    for i in range(1, nrows):
         peer = lax.rem(row + i, nrows)
         pl.semaphore_signal(barrier, inc=1, device_id=(me, peer), device_id_type=MESH)
-        return carry
-
-    lax.fori_loop(1, ntm, hello_tm, 0)
-    lax.fori_loop(1, nrows, hello_rows, 0)
 
     span, nblocks, width = raw.shape
     halves, _, half = wide_in.shape[:3]
@@ -172,15 +171,17 @@
     def entry_at(owner, k):
         return table[owner // per, (owner % per) * pitch + k]
 
-    def fill(o, carry):
-        tiles = [near_out[entry_at(o, k) & (nblocks - 1)] for k in range(slots)]
-        for k in range(slots):
-            wide_out[k // half, o, k % half] = tiles[k]
-        return carry
-
-    lax.fori_loop(0, ntm, fill, 0)
-    for h in range(halves):
+    def fill(h):
+        def place_owner(o, carry):
+            tiles = [near_out[entry_at(o, h * half + k) & (nblocks - 1)] for k in range(half)]
+            for k in range(half):
+                wide_out[h, o, k] = tiles[k]
+            return carry
+
+        lax.fori_loop(0, ntm, place_owner, 0, unroll=2)
         wide_in[h, me] = wide_out[h, me]
+
+    fill(0)
     near_in[me] = near_out[pl.ds(pl.multiple_of(me * near, near), near)]
     pl.semaphore_wait(barrier, ntm + nrows - 2)
 
@@ -195,8 +196,8 @@
         return pltpu.make_async_remote_copy(
             src_ref=wide_out.at[h, peer],
             dst_ref=wide_in.at[h, me],
-            send_sem=wide_send.at[h, peer],
-            recv_sem=wide_recv.at[h, me],
+            send_sem=wide_send.at[h],
+            recv_sem=wide_recv.at[h],
             device_id=(peer, row),
             device_id_type=MESH,
         )
@@ -205,31 +206,26 @@
         return pltpu.make_async_remote_copy(
             src_ref=near_out.at[pl.ds(pl.multiple_of(peer * near, near), near)],
             dst_ref=near_in.at[me],
-            send_sem=near_send.at[peer],
-            recv_sem=near_recv.at[me],
+            send_sem=near_send.at[0],
+            recv_sem=near_recv.at[0],
             device_id=(peer, row),
             device_id_type=MESH,
         )
 
-    def arrival(ref, sem, peer):
-        return pltpu.make_async_remote_copy(
-            src_ref=ref,
-            dst_ref=ref,
-            send_sem=sem,
-            recv_sem=sem,
-            device_id=(peer, row),
-            device_id_type=MESH,
-        )
-
-    def wide_arrival(h, peer):
-        return arrival(wide_in.at[h, peer], wide_recv.at[h, peer], peer)
-
-    def each(body):
-        def step(i, carry):
-            body(lax.rem(me + i, ntm))
-            return carry
-
-        lax.fori_loop(1, ntm, step, 0)
+    def batch(ref, send, recv):
+        return pltpu.make_async_remote_copy(
+            src_ref=ref.at[pl.ds(0, ntm - 1)],
+            dst_ref=ref.at[pl.ds(0, ntm - 1)],
+            send_sem=send,
+            recv_sem=recv,
+            device_id=(lax.rem(me + 1, ntm), row),
+            device_id_type=MESH,
+        )
+
+    def wide_batch(h):
+        return batch(wide_in.at[h], wide_send.at[h], wide_recv.at[h])
+
+    near_batch = batch(near_in, near_send.at[0], near_recv.at[0])
 
     def sum_copy(i):
         peer = lax.rem(row + i, nrows)
@@ -253,11 +249,14 @@
             device_id_type=MESH,
         )
 
+    peers = [peer_at(offset) for offset in order]
     for h in range(halves):
-        for offset in order:
-            wide_copy(h, peer_at(offset)).start()
-    for offset in order:
-        near_copy(peer_at(offset)).start()
+        if h:
+            fill(h)
+        for peer in peers:
+            wide_copy(h, peer).start()
+    for peer in peers:
+        near_copy(peer).start()
 
     nf = ntm * span
     slab_len = nf // nrows
@@ -275,25 +274,23 @@
             )
             for a in range(2)
         ]
-        masks = jnp.concatenate(lines + [jnp.zeros((6, half * width), jnp.float32)], 0)
+        masks = jnp.concatenate(lines + [jnp.zeros((14, half * width), jnp.float32)], 0)
         masks = masks.astype(jnp.bfloat16)
-        each(lambda peer: wide_arrival(h, peer).wait_recv())
+        wide_batch(h).wait_recv()
         pixels = jnp.concatenate([wide_in[h, :, k].reshape(nf, width) for k in range(half)], 1)
-        term = lax.dot_general(masks, pixels, contract, preferred_element_type=jnp.float32)
-        sums_own = term if sums_own is None else sums_own + term
-        if h + 1 == halves:
-            sums_own = sums_own[0:2]
-            sums_ref[row] = sums_own
-            for i in range(1, nrows):
-                sum_copy(i).start()
+        left = jnp.concatenate([pixels * masks[0:1], pixels * masks[1:2], masks], 0)
+        part = lax.dot_general(left, pixels, contract, preferred_element_type=jnp.float32)
         for a in range(2):
-            part = lax.dot_general(
-                pixels * masks[a : a + 1, :], pixels, contract, preferred_element_type=jnp.float32
-            )
+            term = part[a * nf : (a + 1) * nf]
             if h:
-                gram_ref[a] += part
+                gram_ref[a] += term
             else:
-                gram_ref[a] = part
+                gram_ref[a] = term
+        term = part[2 * nf : 2 * nf + 2]
+        sums_own = sums_own + term if h else term
+    sums_ref[row] = sums_own
+    for i in range(1, nrows):
+        sum_copy(i).start()
 
     cycle_all = owner_ref[...] * 2 + slot_ref[...]
     group = lax.broadcasted_iota(jnp.int32, (nrows, 1), 0)
@@ -366,10 +363,8 @@
             code = (value * scale * lines[lane + 4 : lane + 5] + 0.5).astype(jnp.int32) - BIAS
             out_buf[flow, step] = code.astype(jnp.int16)
             ring_copy(flow, step).start()
-        if step == 2:
-            each(lambda peer: arrival(near_in.at[peer], near_recv.at[peer], peer).wait_recv())
-        if step >= 2:
-            lax.fori_loop(2 * step - 4, 2 * step - 2, tau, 0)
+    near_batch.wait_recv()
+    lax.fori_loop(0, near, tau, 0)
 
     for l in range(LEVELS):
         for j in range(lag_ref.shape[1]):
@@ -392,13 +387,22 @@
         two_ref[:, a, :] = total[a] * (count_of(a, behind >= 0) / denom)
 
     for h in range(halves):
-        each(lambda peer: wide_copy(h, peer).wait_send())
-    each(lambda peer: near_copy(peer).wait_send())
+        wide_batch(h).wait_send()
+    near_batch.wait_send()
     for i in range(1, nrows):
         sum_copy(i).wait_send()
     for flow, (a, way, hops) in enumerate(FLOWS):
         for step in range(hops):
             ring_copy(flow, step).wait_send()
+
+
+def finish(g2_ref, two_ref, g2_out, two_out, sem):
+    first = pltpu.make_async_copy(g2_ref, g2_out, sem.at[0])
+    second = pltpu.make_async_copy(two_ref, two_out, sem.at[1])
+    first.start()
+    second.start()
+    first.wait()
+    second.wait()
 
 
 def shards(frames, block_owner, cycle_slot, lag_table):
@@ -417,8 +421,8 @@
     g2, two = pl.pallas_call(
         functools.partial(core, ntm, nrows),
         out_shape=(
-            jax.ShapeDtypeStruct((LEVELS * lag_table.shape[1], near, width), f32),
-            jax.ShapeDtypeStruct((slab, 2, nf), f32),
+            pltpu.VMEM((LEVELS * lag_table.shape[1], near, width), f32),
+            pltpu.VMEM((slab, 2, nf), f32),
         ),
         in_specs=[smem, vmem, vmem, pl.BlockSpec(memory_space=pl.ANY)],
         out_specs=(vmem, vmem),
@@ -440,10 +444,10 @@
             pltpu.VMEM((nflow, STEPS, slab, nf), i16),
             pltpu.VMEM((nflow, STEPS, slab, nf), i16),
             dma((2,)),
-            dma((2, ntm)),
-            dma((2, ntm)),
-            dma((ntm,)),
-            dma((ntm,)),
+            dma((2,)),
+            dma((2,)),
+            dma((1,)),
+            dma((1,)),
             dma((nrows,)),
             dma((nrows,)),
             dma((nflow, STEPS)),
@@ -451,6 +455,16 @@
         ],
         compiler_params=pltpu.CompilerParams(collective_id=0, has_side_effects=True),
     )(lag_table, block_owner[:, :, 0], cycle_slot, frames)
+    g2 = pltpu.with_memory_space_constraint(g2, pltpu.VMEM)
+    two = pltpu.with_memory_space_constraint(two, pltpu.VMEM)
+    hbm = pl.BlockSpec(memory_space=pl.ANY)
+    g2, two = pl.pallas_call(
+        finish,
+        out_shape=(jax.ShapeDtypeStruct(g2.shape, f32), jax.ShapeDtypeStruct(two.shape, f32)),
+        in_specs=[vmem, vmem],
+        out_specs=(hbm, hbm),
+        scratch_shapes=[dma((2,))],
+    )(g2, two)
     return g2[None], two
 
 

time: 57.3 us -> 50.9 us (0.89)
  the two profiles are of different devices: /device:TPU:5 before, /device:TPU:1 now
where the time goes in v4:
time: 50.9 us; the launch traced here: 50.7 us
  Pallas kernels  50.1 us (98%)
  between operations  0.64 us (1%)
    pallas_call x1, Pallas kernels, shards(): pl.pallas_call(functools.partial(core, ntm, nrows), out_shape=(pltpu.VMEM...  49.4 us

profile of v4, /device:TPU:1, one launch (start us, length us, event | category | flops | bytes accessed | tf_op | source)
XLA Modules:
  0.0 50.7 jit_solution(1435802047260026754)
XLA Ops:
  0.6 49.4 %shard_map.59 = (f32[32,4,128]{2,1,0:T(4,128)S(1)}, f32[64,2,512]{2,1,0:T(2,128)S(1)}) custom-call(s32[4,8]{1,0:T(4,128)} %lag_ref.1, s32[8,128]{1,0:T(8,128)} %bitcast.2, s32[8,128]{1,0:T(8,128)} %slot_ref.1, bf16[16,1,128,128]{3,2,1,0:T(8,128)(2,1)} %frames_ref.1), custom_call_target="tpu_custom_call" | custom-call | tf_op jit(solution)/shard_map/pallas_call | solution.py:421
  50.0 0.7 %shard_map.60 = (f32[32,4,128]{2,1,0:T(4,128)}, f32[64,2,512]{2,1,0:T(2,128)}) custom-call(f32[32,4,128]{2,1,0:T(4,128)S(1)} %get-tuple-element.6.g2_ref, f32[64,2,512]{2,1,0:T(2,128)S(1)} %get-tuple-element.7.two_ref), custom_call_target="tpu_custom_call" | custom-call | tf_op jit(solution)/shard_map/pallas_call | solution.py:461

commit v5 on v4

--- a/solution.py
+++ b/solution.py
@@ -11,7 +11,9 @@
 LEVELS = 4
 LAGMAX = 8
 MESH = pl.DeviceIdType.MESH
-FLOWS = ((0, 1, 4), (1, -1, 4), (0, -1, 3), (1, 1, 3))
+PIECES = 1
+CHAINS = ((0, 1, 4), (1, -1, 4), (0, -1, 3), (1, 1, 3))
+FLOWS = tuple((a, way, hops, piece) for piece in range(PIECES) for a, way, hops in CHAINS)
 STEPS = 4
 CODE = 14500.0
 BIAS = 32767
@@ -102,6 +104,7 @@
     gram_ref,
     sums_ref,
     tall_ref,
+    count_ref,
     out_buf,
     in_buf,
     local_sem,
@@ -255,12 +258,34 @@
             fill(h)
         for peer in peers:
             wide_copy(h, peer).start()
-    for peer in peers:
-        near_copy(peer).start()
 
     nf = ntm * span
     slab_len = nf // nrows
     contract = (((1,), (1,)), ((), ()))
+    cycle_all = owner_ref[...] * 2 + slot_ref[...]
+    group = lax.broadcasted_iota(jnp.int32, (nrows, nblocks), 0)
+    distances = [lax.rem(row - group + nrows, nrows), lax.rem(group - row + nrows, nrows)]
+    pixel_counts = [
+        jnp.sum(jnp.where(cycle_all == me * 2 + a, float(width), 0.0), 1, keepdims=True) for a in range(2)
+    ]
+
+    def count_of(d, a, first, last):
+        inside = (distances[d] >= first) & (distances[d] <= last)
+        return jnp.sum(jnp.where(inside, pixel_counts[a], 0.0), 0, keepdims=True)
+
+    def inverse(v):
+        return jnp.where(v > 0, 1.0 / jnp.where(v > 0, v, 1.0), 0.0)
+
+    for step in range(STEPS):
+        before = [inverse(count_of(d, a, 1, step)) * (1.0 / CODE) for d in range(2) for a in range(2)]
+        after = [count_of(d, a, 0, step) * CODE for d in range(2) for a in range(2)]
+        count_ref[step] = jnp.concatenate(before + after, 0)
+    before = [
+        inverse(count_of(d, a, 1, STEPS - (d + a) % 2)) * (1.0 / CODE) for d in range(2) for a in range(2)
+    ]
+    whole = [count_of(0, a, 0, nrows) for a in range(2)]
+    count_ref[STEPS] = jnp.concatenate(before + whole + whole, 0)
+
     own_entries = [entry_at(me, k) // nblocks for k in range(slots)]
     sums_own = None
     for h in range(halves):
@@ -289,36 +314,25 @@
         term = part[2 * nf : 2 * nf + 2]
         sums_own = sums_own + term if h else term
     sums_ref[row] = sums_own
-    for i in range(1, nrows):
+    for i in (1, nrows - 1):
         sum_copy(i).start()
-
-    cycle_all = owner_ref[...] * 2 + slot_ref[...]
-    group = lax.broadcasted_iota(jnp.int32, (nrows, 1), 0)
-    behind = lax.rem(row - group + nrows, nrows)
-    ahead = lax.rem(group - row + nrows, nrows)
-    pixel_counts = [
-        jnp.sum(jnp.where(cycle_all == me * 2 + a, float(width), 0.0), 1, keepdims=True) for a in range(2)
-    ]
-
-    def count_of(a, inside):
-        return jnp.sum(jnp.where(inside, pixel_counts[a], 0.0), 0, keepdims=True)
-
-    def inverse(v):
-        return jnp.where(v > 0, 1.0 / jnp.where(v > 0, v, 1.0), 0.0)
 
     def sums_at(i):
         return sums_ref[lax.rem(row + i, nrows)]
 
-    def tall_at(slab, lane):
-        start = pl.multiple_of(slab * slab_len, slab_len)
-        return tall_ref[pl.ds(start, slab_len), lane : lane + 1]
-
-    def own_part(a, slab):
-        start = pl.multiple_of(slab * slab_len, slab_len)
-        return gram_ref[a, pl.ds(start, slab_len), :]
+    rows_len = slab_len // PIECES
+
+    def rows_at(slab, piece):
+        return pl.ds(pl.multiple_of(slab * slab_len + piece * rows_len, rows_len), rows_len)
+
+    def tall_at(slab, piece, lane):
+        return tall_ref[rows_at(slab, piece), lane : lane + 1]
+
+    def own_part(a, slab, piece):
+        return gram_ref[a, rows_at(slab, piece), :]
 
     def ring_copy(flow, step):
-        _, way, hops = FLOWS[flow]
+        _, way, _, _ = FLOWS[flow]
         return pltpu.make_async_remote_copy(
             src_ref=out_buf.at[flow, step],
             dst_ref=in_buf.at[flow, step],
@@ -332,13 +346,12 @@
         multitau_block(b, near_in, pad_ref, level_ref, corr_ref)
         return carry
 
-    def decode(flow, step, slab, lane, line):
-        a, way, _ = FLOWS[flow]
-        distance = behind if way > 0 else ahead
-        count = count_of(a, (distance >= 1) & (distance <= step))
+    def decode(flow, step, slab, lane, scaled):
+        piece = FLOWS[flow][3]
         value = (in_buf[flow, step - 1].astype(jnp.int32) + BIAS).astype(jnp.float32)
-        return value * (tall_at(slab, lane) * (inverse(count) * (1.0 / CODE))) * line
-
+        return value * tall_at(slab, piece, lane) * scaled[lane : lane + 1]
+
+    rising = lax.rem(row, STEPS) >= STEPS // 2
     up = jnp.zeros_like(sums_own)
     dn = jnp.zeros_like(sums_own)
     for step in range(STEPS):
@@ -349,20 +362,32 @@
             dn = dn + sums_at(step)
         lines = jnp.concatenate([up, dn, inverse(up + sums_own), inverse(dn + sums_own)], 0)
         tall_ref[...] = lines.T
-        for flow, (a, way, hops) in enumerate(FLOWS):
-            if step >= hops:
-                continue
-            slab = lax.rem(row + way * (hops - step) + nrows, nrows)
-            lane = a if way > 0 else 2 + a
-            value = own_part(a, slab)
-            if step:
-                ring_copy(flow, step - 1).wait_recv()
-                value = value + decode(flow, step, slab, lane, lines[lane : lane + 1])
-            count = count_of(a, (behind if way > 0 else ahead) <= step)
-            scale = tall_at(slab, lane + 4) * (count * CODE)
-            code = (value * scale * lines[lane + 4 : lane + 5] + 0.5).astype(jnp.int32) - BIAS
-            out_buf[flow, step] = code.astype(jnp.int16)
-            ring_copy(flow, step).start()
+        scaled = lines * count_ref[step][:, 0:1]
+
+        def serve(way_first, step=step, scaled=scaled):
+            order = list(range(len(FLOWS)))
+            for flow in order:
+                a, way, hops, piece = FLOWS[flow]
+                if step >= hops:
+                    continue
+                slab = lax.rem(row + way * (hops - step) + nrows, nrows)
+                lane = a if way > 0 else 2 + a
+                value = own_part(a, slab, piece)
+                if step:
+                    ring_copy(flow, step - 1).wait_recv()
+                    value = value + decode(flow, step, slab, lane, scaled)
+                scale = tall_at(slab, piece, lane + 4)
+                code = (value * scale * scaled[lane + 4 : lane + 5] + 0.5).astype(jnp.int32) - BIAS
+                out_buf[flow, step] = code.astype(jnp.int16)
+                ring_copy(flow, step).start()
+
+        serve(1)
+        if step == 0:
+            for i in range(2, nrows - 1):
+                sum_copy(i).start()
+            for peer in peers:
+                near_copy(peer).start()
+
     near_batch.wait_recv()
     lax.fori_loop(0, near, tau, 0)
 
@@ -377,21 +402,26 @@
     ends = [up[0:1] + last[0:1], up[1:2], dn[0:1], dn[1:2] + last[1:2]]
     lines = jnp.concatenate(ends + [sums, sums], 0)
     tall_ref[...] = lines.T
-    total = [own_part(a, row) for a in range(2)]
-    for flow, (a, way, hops) in enumerate(FLOWS):
-        ring_copy(flow, hops - 1).wait_recv()
-        lane = a if way > 0 else 2 + a
-        total[a] = total[a] + decode(flow, hops, row, lane, lines[lane : lane + 1])
-    for a in range(2):
-        denom = jnp.maximum(tall_at(row, 4 + a) * sums[a : a + 1], 1.0)
-        two_ref[:, a, :] = total[a] * (count_of(a, behind >= 0) / denom)
+    scaled = lines * count_ref[STEPS][:, 0:1]
+    for piece in range(PIECES):
+        total = [own_part(a, row, piece) for a in range(2)]
+        for flow, (a, way, hops, part) in enumerate(FLOWS):
+            if part != piece:
+                continue
+            ring_copy(flow, hops - 1).wait_recv()
+            lane = a if way > 0 else 2 + a
+            total[a] = total[a] + decode(flow, hops, row, lane, scaled)
+        for a in range(2):
+            denom = jnp.maximum(tall_at(row, piece, 4 + a) * sums[a : a + 1], 1.0)
+            value = total[a] * (count_ref[STEPS, 4 + a : 5 + a, 0:1] / denom)
+            two_ref[pl.ds(piece * rows_len, rows_len), a, :] = value
 
     for h in range(halves):
         wide_batch(h).wait_send()
     near_batch.wait_send()
     for i in range(1, nrows):
         sum_copy(i).wait_send()
-    for flow, (a, way, hops) in enumerate(FLOWS):
+    for flow, (_, _, hops, _) in enumerate(FLOWS):
         for step in range(hops):
             ring_copy(flow, step).wait_send()
 
@@ -441,8 +471,9 @@
             pltpu.VMEM((2, nf, nf), f32),
             pltpu.VMEM((nrows, 2, nf), f32),
             pltpu.VMEM((nf, 8), f32),
-            pltpu.VMEM((nflow, STEPS, slab, nf), i16),
-            pltpu.VMEM((nflow, STEPS, slab, nf), i16),
+            pltpu.VMEM((STEPS + 1, 8, nblocks), f32),
+            pltpu.VMEM((nflow, STEPS, slab // PIECES, nf), i16),
+            pltpu.VMEM((nflow, STEPS, slab // PIECES, nf), i16),
             dma((2,)),
             dma((2,)),
             dma((2,)),

time: 50.9 us -> 48.9 us (0.961)
  the two profiles are of different devices: /device:TPU:1 before, /device:TPU:2 now
where the time goes in v5:
time: 48.9 us; the launch traced here: 48.7 us
  Pallas kernels  48.1 us (98%)
  between operations  0.64 us (1%)
    pallas_call x1, Pallas kernels, shards(): pl.pallas_call(functools.partial(core, ntm, nrows), out_shape=(pltpu.VMEM...  47.4 us

profile of v5, /device:TPU:2, one launch (start us, length us, event | category | flops | bytes accessed | tf_op | source)
XLA Modules:
  0.0 48.7 jit_solution(8409612157321758118)
XLA Ops:
  0.6 47.4 %shard_map.59 = (f32[32,4,128]{2,1,0:T(4,128)S(1)}, f32[64,2,512]{2,1,0:T(2,128)S(1)}) custom-call(s32[4,8]{1,0:T(4,128)} %lag_ref.1, s32[8,128]{1,0:T(8,128)} %bitcast.2, s32[8,128]{1,0:T(8,128)} %slot_ref.1, bf16[16,1,128,128]{3,2,1,0:T(8,128)(2,1)} %frames_ref.1), custom_call_target="tpu_custom_call" | custom-call | tf_op jit(solution)/shard_map/pallas_call | solution.py:451
  48.0 0.7 %shard_map.60 = (f32[32,4,128]{2,1,0:T(4,128)}, f32[64,2,512]{2,1,0:T(2,128)}) custom-call(f32[32,4,128]{2,1,0:T(4,128)S(1)} %get-tuple-element.6.g2_ref, f32[64,2,512]{2,1,0:T(2,128)S(1)} %get-tuple-element.7.two_ref), custom_call_target="tpu_custom_call" | custom-call | tf_op jit(solution)/shard_map/pallas_call | solution.py:492

commit v6 on v5

--- a/solution.py
+++ b/solution.py
@@ -11,7 +11,7 @@
 LEVELS = 4
 LAGMAX = 8
 MESH = pl.DeviceIdType.MESH
-PIECES = 1
+PIECES = 2
 CHAINS = ((0, 1, 4), (1, -1, 4), (0, -1, 3), (1, 1, 3))
 FLOWS = tuple((a, way, hops, piece) for piece in range(PIECES) for a, way, hops in CHAINS)
 STEPS = 4
@@ -105,6 +105,8 @@
     sums_ref,
     tall_ref,
     count_ref,
+    own_buf,
+    ratio_buf,
     out_buf,
     in_buf,
     local_sem,
@@ -122,15 +124,20 @@
     nx = 4
     ny = ntm // (2 * nx)
     barrier = pltpu.get_barrier_semaphore()
+    y, x, c = me // (2 * nx), (me // 2) % nx, me % 2
+
+    def peer_at(offset):
+        dy, dx, dc = offset
+        return (lax.rem(y + dy, ny) * nx + lax.rem(x + dx, nx)) * 2 + lax.rem(c + dc, 2)
+
+    peers = [peer_at(offset) for offset in far_first(ny, nx)]
+    for peer in peers:
+        pl.semaphore_signal(barrier, inc=1, device_id=(peer, row), device_id_type=MESH)
+    for i in sorted(range(1, nrows), key=lambda i: -min(i, nrows - i)):
+        peer = lax.rem(row + i, nrows)
+        pl.semaphore_signal(barrier, inc=1, device_id=(me, peer), device_id_type=MESH)
     load = pltpu.make_async_copy(frames_ref.at[:, 0], raw, local_sem.at[0])
     load.start()
-
-    for i in range(1, ntm):
-        peer = lax.rem(me + i, ntm)
-        pl.semaphore_signal(barrier, inc=1, device_id=(peer, row), device_id_type=MESH)
-    for i in range(1, nrows):
-        peer = lax.rem(row + i, nrows)
-        pl.semaphore_signal(barrier, inc=1, device_id=(me, peer), device_id_type=MESH)
 
     span, nblocks, width = raw.shape
     halves, _, half = wide_in.shape[:3]
@@ -188,13 +195,6 @@
     near_in[me] = near_out[pl.ds(pl.multiple_of(me * near, near), near)]
     pl.semaphore_wait(barrier, ntm + nrows - 2)
 
-    order = far_first(ny, nx)
-    y, x, c = me // (2 * nx), (me // 2) % nx, me % 2
-
-    def peer_at(offset):
-        dy, dx, dc = offset
-        return (lax.rem(y + dy, ny) * nx + lax.rem(x + dx, nx)) * 2 + lax.rem(c + dc, 2)
-
     def wide_copy(h, peer):
         return pltpu.make_async_remote_copy(
             src_ref=wide_out.at[h, peer],
@@ -252,7 +252,6 @@
             device_id_type=MESH,
         )
 
-    peers = [peer_at(offset) for offset in order]
     for h in range(halves):
         if h:
             fill(h)
@@ -346,12 +345,6 @@
         multitau_block(b, near_in, pad_ref, level_ref, corr_ref)
         return carry
 
-    def decode(flow, step, slab, lane, scaled):
-        piece = FLOWS[flow][3]
-        value = (in_buf[flow, step - 1].astype(jnp.int32) + BIAS).astype(jnp.float32)
-        return value * tall_at(slab, piece, lane) * scaled[lane : lane + 1]
-
-    rising = lax.rem(row, STEPS) >= STEPS // 2
     up = jnp.zeros_like(sums_own)
     dn = jnp.zeros_like(sums_own)
     for step in range(STEPS):
@@ -364,24 +357,29 @@
         tall_ref[...] = lines.T
         scaled = lines * count_ref[step][:, 0:1]
 
-        def serve(way_first, step=step, scaled=scaled):
-            order = list(range(len(FLOWS)))
-            for flow in order:
-                a, way, hops, piece = FLOWS[flow]
-                if step >= hops:
-                    continue
-                slab = lax.rem(row + way * (hops - step) + nrows, nrows)
-                lane = a if way > 0 else 2 + a
-                value = own_part(a, slab, piece)
-                if step:
-                    ring_copy(flow, step - 1).wait_recv()
-                    value = value + decode(flow, step, slab, lane, scaled)
-                scale = tall_at(slab, piece, lane + 4)
-                code = (value * scale * scaled[lane + 4 : lane + 5] + 0.5).astype(jnp.int32) - BIAS
+        live = [flow for flow in range(len(FLOWS)) if step < FLOWS[flow][2]]
+        for flow in live:
+            a, way, hops, piece = FLOWS[flow]
+            slab = lax.rem(row + way * (hops - step) + nrows, nrows)
+            lane = a if way > 0 else 2 + a
+            tall = tall_at(slab, piece, lane + 4)
+            line = scaled[lane + 4 : lane + 5]
+            own = own_part(a, slab, piece) * tall * line + 0.5
+            if step:
+                ratio = (tall_at(slab, piece, lane) * tall) * (scaled[lane : lane + 1] * line)
+                ratio_buf[flow] = ratio
+                own_buf[flow] = own + ratio * float(BIAS)
+            else:
+                out_buf[flow, step] = (own.astype(jnp.int32) - BIAS).astype(jnp.int16)
+                ring_copy(flow, step).start()
+        if step:
+            for flow in live:
+                ring_copy(flow, step - 1).wait_recv()
+                value = in_buf[flow, step - 1].astype(jnp.int32).astype(jnp.float32)
+                code = (value * ratio_buf[flow] + own_buf[flow]).astype(jnp.int32) - BIAS
                 out_buf[flow, step] = code.astype(jnp.int16)
                 ring_copy(flow, step).start()
 
-        serve(1)
         if step == 0:
             for i in range(2, nrows - 1):
                 sum_copy(i).start()
@@ -404,16 +402,26 @@
     tall_ref[...] = lines.T
     scaled = lines * count_ref[STEPS][:, 0:1]
     for piece in range(PIECES):
-        total = [own_part(a, row, piece) for a in range(2)]
-        for flow, (a, way, hops, part) in enumerate(FLOWS):
-            if part != piece:
-                continue
-            ring_copy(flow, hops - 1).wait_recv()
-            lane = a if way > 0 else 2 + a
-            total[a] = total[a] + decode(flow, hops, row, lane, scaled)
         for a in range(2):
             denom = jnp.maximum(tall_at(row, piece, 4 + a) * sums[a : a + 1], 1.0)
-            value = total[a] * (count_ref[STEPS, 4 + a : 5 + a, 0:1] / denom)
+            weight = count_ref[STEPS, 4 + a : 5 + a, 0:1] / denom
+            own = own_part(a, row, piece) * weight
+            for d in range(2):
+                flow = FLOWS.index((a, 1 - 2 * d, STEPS - (a + d) % 2, piece))
+                lane = 2 * d + a
+                ratio = tall_at(row, piece, lane) * scaled[lane : lane + 1] * weight
+                ratio_buf[flow] = ratio
+                own = own + ratio * float(BIAS)
+            own_buf[FLOWS.index((a, 1, STEPS - a, piece))] = own
+    for piece in range(PIECES):
+        for a in range(2):
+            value = own_buf[FLOWS.index((a, 1, STEPS - a, piece))]
+            for hops in (STEPS - 1, STEPS):
+                way = 1 if hops == STEPS - a else -1
+                flow = FLOWS.index((a, way, hops, piece))
+                ring_copy(flow, hops - 1).wait_recv()
+                code = in_buf[flow, hops - 1].astype(jnp.int32).astype(jnp.float32)
+                value = value + code * ratio_buf[flow]
             two_ref[pl.ds(piece * rows_len, rows_len), a, :] = value
 
     for h in range(halves):
@@ -472,6 +480,8 @@
             pltpu.VMEM((nrows, 2, nf), f32),
             pltpu.VMEM((nf, 8), f32),
             pltpu.VMEM((STEPS + 1, 8, nblocks), f32),
+            pltpu.VMEM((nflow, slab // PIECES, nf), f32),
+            pltpu.VMEM((nflow, slab // PIECES, nf), f32),
             pltpu.VMEM((nflow, STEPS, slab // PIECES, nf), i16),
             pltpu.VMEM((nflow, STEPS, slab // PIECES, nf), i16),
             dma((2,)),

time: 48.9 us -> 48.1 us (0.984)
  Pallas kernels: 48.1 us -> 47.3 us
    pallas_call x1, Pallas kernels: 47.4 us -> 46.5 us  [shards(): pl.pallas_call(functools.partial(core, ntm, nrows), out_shape=(pltpu.VMEM...]
where the time goes in v6:
time: 48.1 us; the launch traced here: 47.9 us
  Pallas kernels  47.3 us (98%)
  between operations  0.64 us (1%)
    pallas_call x1, Pallas kernels, shards(): pl.pallas_call(functools.partial(core, ntm, nrows), out_shape=(pltpu.VMEM...  46.5 us

profile of v6, /device:TPU:2, one launch (start us, length us, event | category | flops | bytes accessed | tf_op | source)
XLA Modules:
  0.0 47.9 jit_solution(9784240109905128650)
XLA Ops:
  0.6 46.5 %shard_map.59 = (f32[32,4,128]{2,1,0:T(4,128)S(1)}, f32[64,2,512]{2,1,0:T(2,128)S(1)}) custom-call(s32[4,8]{1,0:T(4,128)} %lag_ref.1, s32[8,128]{1,0:T(8,128)} %bitcast.2, s32[8,128]{1,0:T(8,128)} %slot_ref.1, bf16[16,1,128,128]{3,2,1,0:T(8,128)(2,1)} %frames_ref.1), custom_call_target="tpu_custom_call" | custom-call | tf_op jit(solution)/shard_map/pallas_call | solution.py:459
  47.2 0.7 %shard_map.60 = (f32[32,4,128]{2,1,0:T(4,128)}, f32[64,2,512]{2,1,0:T(2,128)}) custom-call(f32[32,4,128]{2,1,0:T(4,128)S(1)} %get-tuple-element.6.g2_ref, f32[64,2,512]{2,1,0:T(2,128)S(1)} %get-tuple-element.7.two_ref), custom_call_target="tpu_custom_call" | custom-call | tf_op jit(solution)/shard_map/pallas_call | solution.py:502

commit v7 on v6

--- a/solution.py
+++ b/solution.py
@@ -15,6 +15,8 @@
 CHAINS = ((0, 1, 4), (1, -1, 4), (0, -1, 3), (1, 1, 3))
 FLOWS = tuple((a, way, hops, piece) for piece in range(PIECES) for a, way, hops in CHAINS)
 STEPS = 4
+FIRST = tuple(sum(flow[2] for flow in FLOWS[:i]) for i in range(len(FLOWS) + 1))
+MESSAGES = FIRST[-1]
 CODE = 14500.0
 BIAS = 32767
 
@@ -124,20 +126,23 @@
     nx = 4
     ny = ntm // (2 * nx)
     barrier = pltpu.get_barrier_semaphore()
+    load = pltpu.make_async_copy(frames_ref.at[:, 0], raw, local_sem.at[0])
+    load.start()
     y, x, c = me // (2 * nx), (me // 2) % nx, me % 2
 
     def peer_at(offset):
         dy, dx, dc = offset
         return (lax.rem(y + dy, ny) * nx + lax.rem(x + dx, nx)) * 2 + lax.rem(c + dc, 2)
 
-    peers = [peer_at(offset) for offset in far_first(ny, nx)]
-    for peer in peers:
+    def wrapped(value, size):
+        return jnp.where(value >= size, value - size, value)
+
+    for i in sorted(range(1, ntm), key=lambda i: -(min(i // 8, 4 - i // 8) + min(i // 2 % 4, 4 - i // 2 % 4))):
+        peer = wrapped(me + i, ntm)
         pl.semaphore_signal(barrier, inc=1, device_id=(peer, row), device_id_type=MESH)
     for i in sorted(range(1, nrows), key=lambda i: -min(i, nrows - i)):
-        peer = lax.rem(row + i, nrows)
+        peer = wrapped(row + i, nrows)
         pl.semaphore_signal(barrier, inc=1, device_id=(me, peer), device_id_type=MESH)
-    load = pltpu.make_async_copy(frames_ref.at[:, 0], raw, local_sem.at[0])
-    load.start()
 
     span, nblocks, width = raw.shape
     halves, _, half = wide_in.shape[:3]
@@ -195,6 +200,8 @@
     near_in[me] = near_out[pl.ds(pl.multiple_of(me * near, near), near)]
     pl.semaphore_wait(barrier, ntm + nrows - 2)
 
+    peers = [peer_at(offset) for offset in far_first(ny, nx)]
+
     def wide_copy(h, peer):
         return pltpu.make_async_remote_copy(
             src_ref=wide_out.at[h, peer],
@@ -235,7 +242,7 @@
         return pltpu.make_async_remote_copy(
             src_ref=sums_ref.at[row],
             dst_ref=sums_ref.at[row],
-            send_sem=sum_send.at[i],
+            send_sem=sum_send.at[0],
             recv_sem=sum_recv.at[row],
             device_id=(me, peer),
             device_id_type=MESH,
@@ -333,10 +340,10 @@
     def ring_copy(flow, step):
         _, way, _, _ = FLOWS[flow]
         return pltpu.make_async_remote_copy(
-            src_ref=out_buf.at[flow, step],
-            dst_ref=in_buf.at[flow, step],
-            send_sem=ring_send.at[flow, step],
-            recv_sem=ring_recv.at[flow, step],
+            src_ref=out_buf.at[FIRST[flow] + step],
+            dst_ref=in_buf.at[FIRST[flow] + step],
+            send_sem=ring_send.at[0],
+            recv_sem=ring_recv.at[FIRST[flow] + step],
             device_id=(me, lax.rem(row + way + nrows, nrows)),
             device_id_type=MESH,
         )
@@ -370,14 +377,14 @@
                 ratio_buf[flow] = ratio
                 own_buf[flow] = own + ratio * float(BIAS)
             else:
-                out_buf[flow, step] = (own.astype(jnp.int32) - BIAS).astype(jnp.int16)
+                out_buf[FIRST[flow] + step] = (own.astype(jnp.int32) - BIAS).astype(jnp.int16)
                 ring_copy(flow, step).start()
         if step:
             for flow in live:
                 ring_copy(flow, step - 1).wait_recv()
-                value = in_buf[flow, step - 1].astype(jnp.int32).astype(jnp.float32)
+                value = in_buf[FIRST[flow] + step - 1].astype(jnp.int32).astype(jnp.float32)
                 code = (value * ratio_buf[flow] + own_buf[flow]).astype(jnp.int32) - BIAS
-                out_buf[flow, step] = code.astype(jnp.int16)
+                out_buf[FIRST[flow] + step] = code.astype(jnp.int16)
                 ring_copy(flow, step).start()
 
         if step == 0:
@@ -420,18 +427,26 @@
                 way = 1 if hops == STEPS - a else -1
                 flow = FLOWS.index((a, way, hops, piece))
                 ring_copy(flow, hops - 1).wait_recv()
-                code = in_buf[flow, hops - 1].astype(jnp.int32).astype(jnp.float32)
+                code = in_buf[FIRST[flow] + hops - 1].astype(jnp.int32).astype(jnp.float32)
                 value = value + code * ratio_buf[flow]
             two_ref[pl.ds(piece * rows_len, rows_len), a, :] = value
 
     for h in range(halves):
         wide_batch(h).wait_send()
     near_batch.wait_send()
-    for i in range(1, nrows):
-        sum_copy(i).wait_send()
-    for flow, (_, _, hops, _) in enumerate(FLOWS):
-        for step in range(hops):
-            ring_copy(flow, step).wait_send()
+    for ref, sem, total in (
+        (sums_ref, sum_send.at[0], nrows - 1),
+        (out_buf, ring_send.at[0], MESSAGES),
+    ):
+        sent = ref.at[pl.ds(0, total)]
+        pltpu.make_async_remote_copy(
+            src_ref=sent,
+            dst_ref=sent,
+            send_sem=sem,
+            recv_sem=sem,
+            device_id=(me, lax.rem(row + 1, nrows)),
+            device_id_type=MESH,
+        ).wait_send()
 
 
 def finish(g2_ref, two_ref, g2_out, two_out, sem):
@@ -482,17 +497,17 @@
             pltpu.VMEM((STEPS + 1, 8, nblocks), f32),
             pltpu.VMEM((nflow, slab // PIECES, nf), f32),
             pltpu.VMEM((nflow, slab // PIECES, nf), f32),
-            pltpu.VMEM((nflow, STEPS, slab // PIECES, nf), i16),
-            pltpu.VMEM((nflow, STEPS, slab // PIECES, nf), i16),
+            pltpu.VMEM((MESSAGES, slab // PIECES, nf), i16),
+            pltpu.VMEM((MESSAGES, slab // PIECES, nf), i16),
             dma((2,)),
             dma((2,)),
             dma((2,)),
             dma((1,)),
             dma((1,)),
+            dma((1,)),
             dma((nrows,)),
-            dma((nrows,)),
-            dma((nflow, STEPS)),
-            dma((nflow, STEPS)),
+            dma((1,)),
+            dma((MESSAGES,)),
         ],
         compiler_params=pltpu.CompilerParams(collective_id=0, has_side_effects=True),
     )(lag_table, block_owner[:, :, 0], cycle_slot, frames)

time: 48.1 us -> 47.6 us (0.990)
  Pallas kernels: 47.3 us -> 46.8 us
where the time goes in v7:
time: 47.6 us; the launch traced here: 47.5 us
  Pallas kernels  46.8 us (98%)
  between operations  0.64 us (1%)
    pallas_call x1, Pallas kernels, shards(): pl.pallas_call(functools.partial(core, ntm, nrows), out_shape=(pltpu.VMEM...  46.1 us

profile of v7, /device:TPU:2, one launch (start us, length us, event | category | flops | bytes accessed | tf_op | source)
XLA Modules:
  0.0 47.5 jit_solution(8213873389065791045)
XLA Ops:
  0.6 46.1 %shard_map.59 = (f32[32,4,128]{2,1,0:T(4,128)S(1)}, f32[64,2,512]{2,1,0:T(2,128)S(1)}) custom-call(s32[4,8]{1,0:T(4,128)} %lag_ref.1, s32[8,128]{1,0:T(8,128)} %bitcast.2, s32[8,128]{1,0:T(8,128)} %slot_ref.1, bf16[16,1,128,128]{3,2,1,0:T(8,128)(2,1)} %frames_ref.1), custom_call_target="tpu_custom_call" | custom-call | tf_op jit(solution)/shard_map/pallas_call | solution.py:474
  46.7 0.7 %shard_map.60 = (f32[32,4,128]{2,1,0:T(4,128)}, f32[64,2,512]{2,1,0:T(2,128)}) custom-call(f32[32,4,128]{2,1,0:T(4,128)S(1)} %get-tuple-element.6.g2_ref, f32[64,2,512]{2,1,0:T(2,128)S(1)} %get-tuple-element.7.two_ref), custom_call_target="tpu_custom_call" | custom-call | tf_op jit(solution)/shard_map/pallas_call | solution.py:517

commit v8 on v7

--- a/solution.py
+++ b/solution.py
@@ -13,7 +13,7 @@
 MESH = pl.DeviceIdType.MESH
 PIECES = 2
 CHAINS = ((0, 1, 4), (1, -1, 4), (0, -1, 3), (1, 1, 3))
-FLOWS = tuple((a, way, hops, piece) for piece in range(PIECES) for a, way, hops in CHAINS)
+FLOWS = tuple((a, way, hops, piece) for a, way, hops in CHAINS for piece in range(PIECES))
 STEPS = 4
 FIRST = tuple(sum(flow[2] for flow in FLOWS[:i]) for i in range(len(FLOWS) + 1))
 MESSAGES = FIRST[-1]

time: 47.6 us -> 46.6 us (0.979)
  Pallas kernels: 46.8 us -> 45.6 us
    pallas_call x1, Pallas kernels: 46.1 us -> 44.9 us  [shards(): pl.pallas_call(functools.partial(core, ntm, nrows), out_shape=(pltpu.VMEM...]
where the time goes in v8:
time: 46.6 us; the launch traced here: 46.3 us
  Pallas kernels  45.6 us (98%)
  between operations  0.64 us (1%)
    pallas_call x1, Pallas kernels, shards(): pl.pallas_call(functools.partial(core, ntm, nrows), out_shape=(pltpu.VMEM...  44.9 us

profile of v8, /device:TPU:2, one launch (start us, length us, event | category | flops | bytes accessed | tf_op | source)
XLA Modules:
  0.0 46.3 jit_solution(12685438227763062808)
XLA Ops:
  0.6 44.9 %shard_map.59 = (f32[32,4,128]{2,1,0:T(4,128)S(1)}, f32[64,2,512]{2,1,0:T(2,128)S(1)}) custom-call(s32[4,8]{1,0:T(4,128)} %lag_ref.1, s32[8,128]{1,0:T(8,128)} %bitcast.2, s32[8,128]{1,0:T(8,128)} %slot_ref.1, bf16[16,1,128,128]{3,2,1,0:T(8,128)(2,1)} %frames_ref.1), custom_call_target="tpu_custom_call" | custom-call | tf_op jit(solution)/shard_map/pallas_call | solution.py:474
  45.5 0.7 %shard_map.60 = (f32[32,4,128]{2,1,0:T(4,128)}, f32[64,2,512]{2,1,0:T(2,128)}) custom-call(f32[32,4,128]{2,1,0:T(4,128)S(1)} %get-tuple-element.6.g2_ref, f32[64,2,512]{2,1,0:T(2,128)S(1)} %get-tuple-element.7.two_ref), custom_call_target="tpu_custom_call" | custom-call | tf_op jit(solution)/shard_map/pallas_call | solution.py:517

commit v9 on v8

--- a/solution.py
+++ b/solution.py
@@ -379,14 +379,18 @@
             else:
                 out_buf[FIRST[flow] + step] = (own.astype(jnp.int32) - BIAS).astype(jnp.int16)
                 ring_copy(flow, step).start()
-        if step:
-            for flow in live:
+        def serve(first, step=step, live=live):
+            for flow in sorted(live, key=lambda f: (-FLOWS[f][2], FLOWS[f][1] != first, f)):
                 ring_copy(flow, step - 1).wait_recv()
                 value = in_buf[FIRST[flow] + step - 1].astype(jnp.int32).astype(jnp.float32)
                 code = (value * ratio_buf[flow] + own_buf[flow]).astype(jnp.int32) - BIAS
                 out_buf[FIRST[flow] + step] = code.astype(jnp.int16)
                 ring_copy(flow, step).start()
 
+        if step:
+            rising = lax.rem(row, STEPS) >= STEPS // 2
+            pl.when(rising)(functools.partial(serve, 1))
+            pl.when(jnp.logical_not(rising))(functools.partial(serve, -1))
         if step == 0:
             for i in range(2, nrows - 1):
                 sum_copy(i).start()

time: 46.6 us -> 46.8 us (level)
  no operation moved by 1% of the time
where the time goes in v9:
time: 46.8 us; the launch traced here: 46.6 us
  Pallas kernels  45.9 us (98%)
  between operations  0.64 us (1%)
    pallas_call x1, Pallas kernels, shards(): pl.pallas_call(functools.partial(core, ntm, nrows), out_shape=(pltpu.VMEM...  45.2 us

profile of v9, /device:TPU:2, one launch (start us, length us, event | category | flops | bytes accessed | tf_op | source)
XLA Modules:
  0.0 46.6 jit_solution(5164486798599267936)
XLA Ops:
  0.6 45.2 %shard_map.59 = (f32[32,4,128]{2,1,0:T(4,128)S(1)}, f32[64,2,512]{2,1,0:T(2,128)S(1)}) custom-call(s32[4,8]{1,0:T(4,128)} %lag_ref.1, s32[8,128]{1,0:T(8,128)} %bitcast.2, s32[8,128]{1,0:T(8,128)} %slot_ref.1, bf16[16,1,128,128]{3,2,1,0:T(8,128)(2,1)} %frames_ref.1), custom_call_target="tpu_custom_call" | custom-call | tf_op jit(solution)/shard_map/pallas_call | solution.py:478
  45.8 0.7 %shard_map.60 = (f32[32,4,128]{2,1,0:T(4,128)}, f32[64,2,512]{2,1,0:T(2,128)}) custom-call(f32[32,4,128]{2,1,0:T(4,128)S(1)} %get-tuple-element.6.g2_ref, f32[64,2,512]{2,1,0:T(2,128)S(1)} %get-tuple-element.7.two_ref), custom_call_target="tpu_custom_call" | custom-call | tf_op jit(solution)/shard_map/pallas_call | solution.py:521
